TPU v7x, 512 devices: a whole 4x4x16 slice. The times are simulated.
512 devices in a mesh: tok: 16 (over y, x), hid: 32 (over z, core).
Axes of the slice: x: 4, y: 4, z: 16, core: 2. Of those that a mesh axis runs over, the one named last changes fastest.
Arguments:
- tokens: bfloat16 [2048, 8192], P('tok', 'hid'), may hold values from -6 to 6
- gate_weight: bfloat16 [8192, 16384], P('tok', 'hid'), may hold values from -0.09375 to 0.09375
- up_weight: bfloat16 [8192, 16384], P('tok', 'hid'), may hold values from -0.09375 to 0.09375
- down_weight: bfloat16 [16384, 8192], P('hid', 'tok'), may hold values from -0.0625 to 0.0625
- gate_keep: int32 [64, 128], P('tok', 'hid'), may hold values from 0 to 1, as said below
- up_keep: int32 [64, 128], P('tok', 'hid'), may hold values from 0 to 1, as said below
- down_keep: int32 [128, 64], P('hid', 'tok'), may hold values from 0 to 1, as said below
Outputs:
- mixed: bfloat16 [2048, 8192], P('hid', 'tok')
Inputs may be any that keep to these rules, and one draw needn't show every extreme that they name: `gate_keep`: in every device's shard of 4 x 4 blocks of a mask, between 4 and 8 blocks are kept; in every mask some shard keeps exactly 8. Shards of down_keep are 4 x 4. `up_keep`: as for gate_keep, drawn independently. `down_keep`: as for gate_keep, drawn independently.
All inputs are finite; a program needn't handle non-finite values.
Results may differ from a plain program's by a relative error of at most 0.0049.
Values may be sent and summed in bfloat16 or wider, within the bound.
A program may use at most 64 MiB of HBM per device.

v0:
```python
import jax
import jax.numpy as jnp
from jax import lax
from jax.sharding import PartitionSpec as P


def pack_blocks(weight, keep_mask):
    block_rows, block_cols = keep_mask.shape
    side = weight.shape[0] // block_rows
    capacity = block_rows * block_cols // 2
    flat_keep = keep_mask.reshape(-1)
    block_rank = jnp.cumsum(flat_keep) - 1
    slot_ids = jnp.arange(capacity, dtype=jnp.int32)
    select = ((block_rank[None, :] == slot_ids[:, None]) & (flat_keep[None, :] == 1)).astype(
        weight.dtype
    )
    blocks = weight.reshape(block_rows, side, block_cols, side).transpose(0, 2, 1, 3)
    blocks = blocks.reshape(block_rows * block_cols, side, side)
    packed = jnp.einsum("sb,bij->sij", select, blocks, preferred_element_type=jnp.float32)
    return (packed.astype(weight.dtype)[None], flat_keep[None])


def unpack_blocks(packed, flags, block_rows, block_cols):
    shards, capacity, side, _ = packed.shape
    block_rank = jnp.cumsum(flags, axis=1) - 1
    slot_ids = jnp.arange(capacity, dtype=jnp.int32)
    select = (
        (block_rank[:, :, None] == slot_ids[None, None, :]) & (flags[:, :, None] == 1)
    ).astype(packed.dtype)
    dense_tiles = jnp.einsum(
        "kbs,ksij->kbij", select, packed, preferred_element_type=jnp.float32
    ).astype(packed.dtype)
    dense_tiles = dense_tiles.reshape(shards, block_rows, block_cols, side, side).transpose(
        0, 1, 3, 2, 4
    )
    return dense_tiles.reshape(shards * block_rows * side, block_cols * side)


def prune_local(weight, keep_mask):
    block_rows, block_cols = keep_mask.shape
    row_count, col_count = weight.shape
    tiles = weight.reshape(block_rows, row_count // block_rows, block_cols, col_count // block_cols)
    kept = tiles * keep_mask[:, None, :, None].astype(weight.dtype)
    return kept.reshape(row_count, col_count)


def local(tokens, gate_weight, up_weight, down_weight, gate_keep, up_keep, down_keep):
    features_all = lax.all_gather(tokens, "hid", axis=1, tiled=True)
    block_rows, block_cols = gate_keep.shape
    gate_packed, gate_flags = pack_blocks(gate_weight, gate_keep)
    up_packed, up_flags = pack_blocks(up_weight, up_keep)

    def add_product(packed, flags):
        dense_strip = unpack_blocks(packed, flags, block_rows, block_cols)
        return jnp.dot(features_all, dense_strip, preferred_element_type=jnp.float32)

    def add_single(arrived):
        return add_product(arrived[0], arrived[1])

    gate_out = add_single(
        (
            lax.all_gather(gate_packed, "tok", axis=0, tiled=True),
            lax.all_gather(gate_flags, "tok", axis=0, tiled=True),
        )
    )
    up_out = add_single(
        (
            lax.all_gather(up_packed, "tok", axis=0, tiled=True),
            lax.all_gather(up_flags, "tok", axis=0, tiled=True),
        )
    )
    hidden = (jax.nn.silu(gate_out) * up_out).astype(jnp.bfloat16)
    down_dense = prune_local(down_weight, down_keep)
    partial_sums = jnp.dot(
        lax.all_gather(hidden, "tok", axis=0, tiled=True),
        down_dense,
        preferred_element_type=jnp.float32,
    )
    mixed = lax.psum_scatter(partial_sums, "hid", scatter_dimension=0, tiled=True)
    return mixed.astype(jnp.bfloat16)


def solution(mesh):
    return jax.shard_map(
        local,
        mesh=mesh,
        in_specs=(
            P("tok", "hid"),
            P("tok", "hid"),
            P("tok", "hid"),
            P("hid", "tok"),
            P("tok", "hid"),
            P("tok", "hid"),
            P("hid", "tok"),
        ),
        out_specs=P("hid", "tok"),
        check_vma=False,
    )
```

profile of v0, /device:TPU:6, one launch (start us, length us, event | category | flops | bytes accessed | tf_op | source)
XLA Modules:
  0.0 432.7 jit_solution(12943204567747657550)
XLA Ops:
  6.5 0.0 all-gather.13.cloned.1.call-start
  6.5 0.8 reshape.145
  7.4 0.7 broadcast_compare_fusion.3
  8.1 1.2 reshape.124
  9.2 0.2 copy.25
  9.4 0.1 add_reduce_fusion.1
  9.6 0.1 eq.90
  9.7 0.9 convolution_convert_fusion.3
  10.6 0.0 all-gather.13.cloned.1.call-update
  10.6 0.0 all-gather.15.cloned.1.call-start
  10.7 1.2 reshape.129
  11.8 0.2 copy.29
  12.0 0.0 copy-done.3
  12.0 0.1 reshape.146
  12.2 0.1 eq.99
  12.3 0.1 add_reduce_fusion
  12.4 0.9 convolution_convert_fusion.2
  13.3 0.0 all-gather.15.cloned.1.call-update
  13.3 0.0 all-gather.9.cloned.1.call-start
  13.4 0.7 all-gather.9.cloned.1.call-update
  14.1 0.0 all-gather.11.cloned.1.call-start
  14.1 0.0 copy-done.2
  14.1 0.1 reshape.135
  14.2 0.1 reshape.137
  14.3 22.8 %all-gather.2 = s32[16,1,16]{2,1,0:T(1,128)S(1)} all-gather(s32[1,1,16]{2,1,0:T(1,128)S(1)} %reshape.135), channel_id=1, replica_groups=mesh['tok'=16,'hid'=32] {'tok'}, dimensions={0}, use_global_device_ids=true | all-gather | bytes 1088 | tf_op jit(solution)/shard_map/all_gather | solution.py:63
  37.1 0.2 reduce_window_sum.26
  37.3 17.0 %all-gather.3 = s32[16,1,16]{2,1,0:T(1,128)S(1)} all-gather(s32[1,1,16]{2,1,0:T(1,128)S(1)} %reshape.137), channel_id=1, replica_groups=mesh['tok'=16,'hid'=32] {'tok'}, dimensions={0}, use_global_device_ids=true | all-gather | bytes 1088 | tf_op jit(solution)/shard_map/all_gather | solution.py:69
  54.3 0.2 reduce_window_sum.27
  54.5 32.5 %all-gather.13.cloned.1.call-done = bf16[128,128,128]{2,0,1:T(8,128)(2,1)} async-done(((bf16[8,128,128]{2,0,1:T(8,128)(2,1)}), bf16[128,128,128]{2,0,1:T(8,128)(2,1)}) %all-gather.13.cloned.1.call-update) | async-done | bytes 4194320 | tf_op jit(solution)/shard_map/all_gather | solution.py:62
  87.0 4.2 convolution_convert_fusion.1
  91.2 5.9 %copy.27 = bf16[16,4,4,128,128]{4,2,3,1,0:T(4,128)(2,1)} copy(bf16[16,4,4,128,128]{4,2,1,3,0:T(4,128)(2,1)S(1)} %bitcast.70) | data formatting | bytes 16777216 | tf_op jit(solution)/shard_map/reshape | solution.py:33
  97.1 64.5 %all-gather.15.cloned.1.call-done = bf16[128,128,128]{2,0,1:T(8,128)(2,1)} async-done(((bf16[8,128,128]{2,0,1:T(8,128)(2,1)}), bf16[128,128,128]{2,0,1:T(8,128)(2,1)}) %all-gather.15.cloned.1.call-update) | async-done | bytes 4194320 | tf_op jit(solution)/shard_map/all_gather | solution.py:68
  161.6 4.2 convolution_convert_fusion
  165.9 5.9 %copy.31 = bf16[16,4,4,128,128]{4,2,3,1,0:T(4,128)(2,1)} copy(bf16[16,4,4,128,128]{4,2,1,3,0:T(4,128)(2,1)S(1)} %bitcast.71) | data formatting | bytes 16777216 | tf_op jit(solution)/shard_map/reshape | solution.py:33
  171.8 64.5 %all-gather.9.cloned.1.call-done = bf16[128,8192]{1,0:T(8,128)(2,1)} async-done(((bf16[128,256]{1,0:T(8,128)(2,1)}), bf16[128,8192]{1,0:T(8,128)(2,1)}) %all-gather.9.cloned.1.call-update) | async-done | bytes 2097168 | tf_op jit(solution)/shard_map/all_gather | solution.py:48
  236.3 6.5 %fusion.8 = f32[128,512]{0,1:T(8,128)S(1)} fusion(bf16[128,8192]{1,0:T(8,128)(2,1)} %all-gather.9.cloned.1.call-done, bf16[1024,8,4,128]{3,2,1,0:T(4,128)(2,1)} %bitcast.72), kind=kOutput, calls=%fused_computation.12 | convolution fusion | flops 1073741824 | bytes 10747904 | tf_op jit(solution)/shard_map/dot_general | solution.py:55
  242.8 0.0 copy-done
  242.8 0.5 copy-done.5
  243.3 3.2 fusion.17
  246.5 0.0 all-gather.11.cloned.1.call-update
  246.5 0.0 reduce-scatter.2.cloned.1.call-start
  246.6 0.0 copy-done.4
  246.6 58.0 %all-gather.11.cloned.1.call-done = bf16[2048,512]{0,1:T(8,128)(2,1)} async-done(((bf16[128,512]{0,1:T(8,128)(2,1)}), bf16[2048,512]{0,1:T(8,128)(2,1)}) %all-gather.11.cloned.1.call-update) | async-done | bytes 2097168 | tf_op jit(solution)/shard_map/all_gather | solution.py:75
  304.6 0.2 mul.20
  304.8 4.8 %fusion.20 = f32[2048,512]{1,0:T(8,128)} fusion(bf16[2048,512]{0,1:T(8,128)(2,1)} %all-gather.11.cloned.1.call-done, bf16[512,512]{1,0:T(8,128)(2,1)S(1)} %copy-done.1, bf16[64,8,4,128]{3,2,1,0:T(4,128)(2,1)S(1)} %bitcast.74), kind=kOutput, calls=%fused_computation.17 | convolution fusion | flops 1074003968 | bytes 7340032 | tf_op jit(solution)/shard_map/dot_general | solution.py:74
  309.6 0.0 reduce-scatter.2.cloned.1.call-update
  309.7 115.0 %reduce-scatter.2.cloned.1.call-done = f32[64,512]{1,0:T(8,128)} async-done(((f32[2048,512]{1,0:T(8,128)}), f32[64,512]{1,0:T(8,128)}) %reduce-scatter.2.cloned.1.call-update) | async-done | bytes 131088 | tf_op jit(solution)/shard_map/reduce_scatter | solution.py:79
  424.7 1.5 convert_element_type.32
  (15 shorter events, 0.1 us)
Async XLA Ops:
  6.5 7.6 %copy-start.2 = (s32[4,4]{1,0:T(4,128)S(1)}, s32[4,4]{1,0:T(4,128)}, u32[]{:S(2)}) copy-start(s32[4,4]{1,0:T(4,128)} %param.11) | copy-start | bytes 196
  6.5 5.5 %copy-start.3 = (s32[4,4]{1,0:T(4,128)S(1)}, s32[4,4]{1,0:T(4,128)}, u32[]{:S(2)}) copy-start(s32[4,4]{1,0:T(4,128)} %param.12) | copy-start | bytes 196
  6.5 80.5 %all-gather.13.cloned.1.call-start = ((), (), s32[]{:S(2)}) async-start(), calls=%async_computation.4 | async-start | bytes 4456448 | tf_op jit(solution)/shard_map/all_gather | solution.py:62
  10.6 151.0 %all-gather.15.cloned.1.call-start = ((), (), s32[]{:S(2)}) async-start(), calls=%async_computation.5 | async-start | bytes 4456448 | tf_op jit(solution)/shard_map/all_gather | solution.py:68
  13.3 223.0 %all-gather.9.cloned.1.call-start = ((), (), s32[]{:S(2)}) async-start(), calls=%async_computation.1 | async-start | bytes 2162688 | tf_op jit(solution)/shard_map/all_gather | solution.py:48
  14.1 290.5 %all-gather.11.cloned.1.call-start = ((), (), s32[]{:S(2)}) async-start(), calls=%async_computation.2 | async-start | bytes 2228224 | tf_op jit(solution)/shard_map/all_gather | solution.py:75
  236.3 6.5 %copy-start = (bf16[16,4,4,128,128]{4,2,3,1,0:T(4,128)(2,1)S(1)}, bf16[16,4,4,128,128]{4,2,3,1,0:T(4,128)(2,1)}, u32[]{:S(2)}) copy-start(bf16[16,4,4,128,128]{4,2,3,1,0:T(4,128)(2,1)} %copy.31) | copy-start | bytes 25165828
  236.3 7.0 %copy-start.5 = (bf16[128,8192]{1,0:T(8,128)(2,1)S(1)}, bf16[128,8192]{1,0:T(8,128)(2,1)}, u32[]{:S(2)}) copy-start(bf16[128,8192]{1,0:T(8,128)(2,1)} %all-gather.9.cloned.1.call-done) | copy-start | bytes 6291460
  243.3 3.3 copy-start.4
  243.3 61.5 %copy-start.1 = (bf16[512,512]{1,0:T(8,128)(2,1)S(1)}, bf16[512,512]{1,0:T(8,128)(2,1)}, u32[]{:S(2)}) copy-start(bf16[512,512]{1,0:T(8,128)(2,1)} %param.10) | copy-start | bytes 1572868
  246.5 178.1 %reduce-scatter.2.cloned.1.call-start = ((), (), s32[]{:S(2)}) async-start(), calls=%async_computation.3 | async-start | bytes 4325376 | tf_op jit(solution)/shard_map/reduce_scatter | solution.py:79
Sparse Core Ops, SparseCore 0:
  10.7 76.2 all-gather.12
  90.0 71.5 all-gather.14
  163.7 72.5 all-gather.8
  246.7 57.8 all-gather.10
  309.8 114.8 reduce-scatter.1
where the time goes:
time: 434 us; the launch traced here: 433 us
  waiting for transfers between devices  335 us (77%)
  blocking collectives  39.9 us (9%)
  matrix products  24.9 us (6%)
  local copies, waits for them, and re-layouts  16.4 us (4%)
  between operations  13.3 us (3%)
    reduce_scatter x1, waiting for transfers between devices, local(): lax.psum_scatter(partial_sums, 'hid', scatter_dimension=0, tiled=True)  115 us
    all_gather x1, waiting for transfers between devices, local(): features_all = lax.all_gather(tokens, 'hid', axis=1, tiled=True)  64.5 us
    all_gather x1, waiting for transfers between devices, local(): lax.all_gather(up_packed, 'tok', axis=0, tiled=True)  64.5 us
    all_gather x1, waiting for transfers between devices, local(): lax.all_gather(hidden, 'tok', axis=0, tiled=True)  58 us
    all_gather x1, waiting for transfers between devices, local(): lax.all_gather(gate_packed, 'tok', axis=0, tiled=True)  32.5 us
    all_gather x1, blocking collectives, local(): lax.all_gather(gate_flags, 'tok', axis=0, tiled=True)  22.8 us
    all_gather x1, blocking collectives, local(): lax.all_gather(up_flags, 'tok', axis=0, tiled=True)  17 us
    reshape x2, local copies, waits for them, and re-layouts, unpack_blocks(): dense_tiles.reshape(shards, block_rows, block_cols, side, side)  11.8 us
  transfers between devices with their start and end apart: 5, of which 5 were waited for; matrix products, arithmetic and copies ran while one was open for 5% of the time, Pallas kernels for 0%

commit v1 on v0

v1 whole, which is shorter than its diff:
```python
import functools

import jax
import jax.numpy as jnp
from jax import lax
from jax.experimental import pallas as pl
from jax.experimental.pallas import tpu as pltpu
from jax.sharding import PartitionSpec as P

MESH = pl.DeviceIdType.MESH
HBM = pltpu.MemorySpace.HBM
VMEM = pltpu.MemorySpace.VMEM
BF16 = jnp.bfloat16
F32 = jnp.float32

SIDE = 4
RING = 16
BLK = 128
NB = 4
CAP = 8
SHARD = NB * BLK
PACK = CAP * BLK + 16
HALF = CAP * BLK // 2


def place():
    t = lax.axis_index("tok")
    h = lax.axis_index("hid")
    return lax.rem(t, SIDE), lax.div(t, SIDE), lax.div(h, 2), lax.rem(h, 2)


def wrap(i, n):
    return lax.rem(i + n, n)


def device(x, y, z, c):
    return (y * SIDE + x, z * 2 + c)


def greet(peers):
    barrier = pltpu.get_barrier_semaphore()
    for peer in peers:
        pl.semaphore_signal(barrier, inc=1, device_id=peer, device_id_type=MESH)
    pl.semaphore_wait(barrier, len(peers))


class Gather:
    def __init__(self, buf, half, x_first, send, recv):
        x, y, z, c = place()
        self.buf, self.half, self.send, self.recv = buf, half, send, recv
        self.a, self.b = (x, y) if x_first else (y, x)
        self.slot = lambda a, b: (b * SIDE + a) if x_first else (a * SIDE + b)
        self.dev = lambda a, b: device(a, b, z, c) if x_first else device(b, a, z, c)
        self.copies = {}

    def part(self, slot, piece):
        ref = self.buf.at[slot]
        if piece is None:
            return ref
        return ref.at[self.half] if piece == 0 else ref.at[self.half2]

    def block(self, k, piece):
        a = wrap(self.a + k, SIDE)
        return a, piece

    def copy(self, key, index, slot, piece, dev):
        ref = self.part(slot, piece)
        cp = pltpu.make_async_remote_copy(
            src_ref=ref,
            dst_ref=ref,
            send_sem=self.send.at[index],
            recv_sem=self.recv.at[index],
            device_id=dev,
            device_id_type=MESH,
        )
        cp.start()
        self.copies[key] = cp

    def got(self, index, slot, piece):
        ref = self.part(slot, piece)
        x, y, z, c = place()
        pltpu.make_async_remote_copy(
            src_ref=ref,
            dst_ref=ref,
            send_sem=self.send.at[index],
            recv_sem=self.recv.at[index],
            device_id=self.dev(wrap(self.a + 1, SIDE), self.b),
            device_id_type=MESH,
        ).wait_recv()

    def first(self):
        s = self.slot(self.a, self.b)
        self.copy("r", 0, s, None, self.dev(wrap(self.a + 1, SIDE), self.b))
        self.copy("l", 1, s, None, self.dev(wrap(self.a - 1, SIDE), self.b))

    def relay(self):
        left = self.slot(wrap(self.a - 1, SIDE), self.b)
        right = self.slot(wrap(self.a + 1, SIDE), self.b)
        self.got(0, left, None)
        self.copy("fr", 2, left, 0, self.dev(wrap(self.a + 1, SIDE), self.b))
        self.got(1, right, None)
        self.copy("fl", 3, right, 1, self.dev(wrap(self.a - 1, SIDE), self.b))

    def far(self):
        opposite = self.slot(wrap(self.a + 2, SIDE), self.b)
        self.got(2, opposite, 0)
        self.got(3, opposite, 1)

    OFF = (0, -1, 1, 2)

    def second(self, i):
        a = wrap(self.a + self.OFF[i], SIDE)
        s = self.slot(a, self.b)
        self.copy(("u", i), 4 + 4 * i, s, None, self.dev(self.a, wrap(self.b + 1, SIDE)))
        self.copy(("d", i), 5 + 4 * i, s, None, self.dev(self.a, wrap(self.b - 1, SIDE)))

    def relay2(self, i):
        a = wrap(self.a + self.OFF[i], SIDE)
        below = self.slot(a, wrap(self.b - 1, SIDE))
        above = self.slot(a, wrap(self.b + 1, SIDE))
        self.got(4 + 4 * i, below, None)
        self.copy(("fu", i), 6 + 4 * i, below, 0, self.dev(self.a, wrap(self.b + 1, SIDE)))
        self.got(5 + 4 * i, above, None)
        self.copy(("fd", i), 7 + 4 * i, above, 1, self.dev(self.a, wrap(self.b - 1, SIDE)))

    def far2(self, i):
        a = wrap(self.a + self.OFF[i], SIDE)
        s = self.slot(a, wrap(self.b + 2, SIDE))
        self.got(6 + 4 * i, s, 0)
        self.got(7 + 4 * i, s, 1)

    def drain(self):
        for cp in self.copies.values():
            cp.wait_send()


def halves(gather, first, second):
    gather.half, gather.half2 = first, second
    return gather


def pack_kernel(at_ref, gk_ref, uk_ref, dk_ref, tok_ref, gw_ref, uw_ref, dw_ref, g_ref, u_ref, t_ref, d_ref):
    del at_ref
    t_ref[0] = tok_ref[...]
    lane = lax.broadcasted_iota(jnp.int32, (16, BLK), 1)
    for keep_ref, w_ref, o_ref in ((gk_ref, gw_ref, g_ref), (uk_ref, uw_ref, u_ref)):
        o_ref[...] = jnp.zeros_like(o_ref)
        rank = jnp.int32(0)
        flags = jnp.zeros((16, BLK), F32)
        for b in range(NB * NB):
            i, j = b // NB, b % NB
            keep = keep_ref[i, j]

            @pl.when(keep == 1)
            def _(i=i, j=j, rank=rank, w_ref=w_ref, o_ref=o_ref):
                row = pl.multiple_of(jnp.minimum(rank, CAP - 1) * BLK, BLK)
                o_ref[0, pl.ds(row, BLK), :] = w_ref[i * BLK : (i + 1) * BLK, j * BLK : (j + 1) * BLK]

            flags = jnp.where(lane == b, keep.astype(F32), flags)
            rank = rank + keep
        o_ref[0, CAP * BLK :, :] = flags.astype(BF16)
    for i in range(NB):
        for j in range(NB):
            r, s = slice(i * BLK, (i + 1) * BLK), slice(j * BLK, (j + 1) * BLK)
            d_ref[0, r, s] = dw_ref[r, s] * dk_ref[i, j].astype(F32).astype(BF16)


def pack(at, tokens, gw, uw, dw, gk, uk, dk):
    whole = lambda a: pl.BlockSpec(a.shape, lambda i, *_: (0,) * a.ndim)
    return pl.pallas_call(
        pack_kernel,
        grid_spec=pltpu.PrefetchScalarGridSpec(
            num_scalar_prefetch=4,
            grid=(1,),
            in_specs=[whole(a) for a in (tokens, gw, uw, dw)],
            out_specs=[
                pl.BlockSpec((1, PACK, BLK), lambda i, at, *_: (at[0], 0, 0)),
                pl.BlockSpec((1, PACK, BLK), lambda i, at, *_: (at[0], 0, 0)),
                pl.BlockSpec((1,) + tokens.shape, lambda i, at, *_: (at[1], 0, 0)),
                pl.BlockSpec((1,) + dw.shape, lambda i, at, *_: (at[2], 0, 0)),
            ],
        ),
        out_shape=[
            jax.ShapeDtypeStruct((SIDE * SIDE, PACK, BLK), BF16),
            jax.ShapeDtypeStruct((SIDE * SIDE, PACK, BLK), BF16),
            jax.ShapeDtypeStruct((2 * RING,) + tokens.shape, BF16),
            jax.ShapeDtypeStruct((2,) + dw.shape, BF16),
        ],
        name="pack",
    )(at, gk, uk, dk, tokens, gw, uw, dw)


def gather_kernel(g_in, u_in, t_in, d_in, g, u, t, d, gs, gr, us, ur, zs, zr, cs, cr, ds, dr):
    del g_in, u_in, t_in, d_in
    x, y, z, c = place()
    up, down = device(x, y, wrap(z + 1, RING), c), device(x, y, wrap(z - 1, RING), c)
    other = device(x, y, z, 1 - c)
    greet(
        (
            device(wrap(x + 1, SIDE), y, z, c),
            device(wrap(x - 1, SIDE), y, z, c),
            device(x, wrap(y + 1, SIDE), z, c),
            device(x, wrap(y - 1, SIDE), z, c),
            up,
            down,
            other,
        )
    )
    first, second = pl.ds(0, HALF), pl.ds(HALF, PACK - HALF)
    gg = halves(Gather(g, None, True, gs, gr), first, second)
    uu = halves(Gather(u, None, False, us, ur), first, second)
    sends = []

    def z_copy(block, dev, send, recv, start):
        ref = t.at[2 * block + c]
        cp = pltpu.make_async_remote_copy(
            src_ref=ref, dst_ref=ref, send_sem=send, recv_sem=recv, device_id=dev, device_id_type=MESH
        )
        if start:
            cp.start()
            sends.append(cp)
        else:
            cp.wait_recv()

    def z_step(k):
        z_copy(wrap(z - (k - 1), RING), up, zs.at[2 * k - 2], zr.at[2 * k - 2], True)
        if k < RING // 2:
            z_copy(wrap(z + (k - 1), RING), down, zs.at[2 * k - 1], zr.at[2 * k - 1], True)

    def z_wait(k):
        z_copy(wrap(z - k, RING), up, zs.at[2 * k - 2], zr.at[2 * k - 2], False)
        z_copy(wrap(z - k, RING), other, cs.at[2 * k - 1], cr.at[2 * k - 1], True)
        if k < RING // 2:
            z_copy(wrap(z + k, RING), down, zs.at[2 * k - 1], zr.at[2 * k - 1], False)
            z_copy(wrap(z + k, RING), other, cs.at[2 * k], cr.at[2 * k], True)

    def z_go(k):
        z_wait(k)
        if k < RING // 2:
            z_step(k + 1)

    z_step(1)
    gg.first()
    uu.first()
    gg.second(0)
    uu.second(0)
    z_copy(z, other, cs.at[0], cr.at[0], True)
    dref = d.at[c]
    d_copy = pltpu.make_async_remote_copy(
        src_ref=dref, dst_ref=dref, send_sem=ds.at[0], recv_sem=dr.at[0], device_id=other, device_id_type=MESH
    )
    d_copy.start()
    z_go(1)
    z_go(2)
    gg.relay()
    uu.relay()
    gg.second(1)
    uu.second(1)
    gg.second(2)
    uu.second(2)
    z_go(3)
    gg.relay2(0)
    uu.relay2(0)
    z_go(4)
    gg.far()
    uu.far()
    gg.second(3)
    uu.second(3)
    z_go(5)
    gg.relay2(1)
    uu.relay2(1)
    z_go(6)
    gg.relay2(2)
    uu.relay2(2)
    z_go(7)
    gg.far2(0)
    uu.far2(0)
    z_go(8)
    gg.relay2(3)
    uu.relay2(3)
    for i in (1, 2, 3):
        gg.far2(i)
        uu.far2(i)
    for n in range(RING):
        k = (n + 1) // 2
        block = z if n == 0 else (wrap(z - k, RING) if n % 2 else wrap(z + k, RING))
        ref = t.at[2 * block + 1 - c]
        pltpu.make_async_remote_copy(
            src_ref=ref, dst_ref=ref, send_sem=cs.at[n], recv_sem=cr.at[n], device_id=other, device_id_type=MESH
        ).wait_recv()
    oref = d.at[1 - c]
    pltpu.make_async_remote_copy(
        src_ref=oref, dst_ref=oref, send_sem=ds.at[0], recv_sem=dr.at[0], device_id=other, device_id_type=MESH
    ).wait_recv()
    d_copy.wait_send()
    gg.drain()
    uu.drain()
    for cp in sends:
        cp.wait_send()


def gather_weights(g, u, t, d):
    dma = pltpu.SemaphoreType.DMA
    arrays = (g, u, t, d)
    return pl.pallas_call(
        gather_kernel,
        out_shape=[jax.ShapeDtypeStruct(a.shape, a.dtype) for a in arrays],
        in_specs=[pl.BlockSpec(memory_space=HBM)] * 4,
        out_specs=[pl.BlockSpec(memory_space=HBM)] * 4,
        input_output_aliases={i: i for i in range(4)},
        scratch_shapes=[dma((20,))] * 4 + [dma((15,))] * 2 + [dma((16,))] * 2 + [dma((1,))] * 2,
        compiler_params=pltpu.CompilerParams(collective_id=0, has_side_effects=True),
        name="gather_weights",
    )(*arrays)


def hidden_kernel(flag_ref, at_ref, g_ref, u_ref, t_ref, own_ref, other_ref, gd, ud, ga, ua):
    s = pl.program_id(0)

    @pl.when(s == 0)
    def _():
        ga[...] = jnp.zeros_like(ga)
        ua[...] = jnp.zeros_like(ua)

    for m, (packed, dense, acc) in enumerate(((g_ref, gd, ga), (u_ref, ud, ua))):
        rank = jnp.int32(0)
        for b in range(NB * NB):
            i, j = b // NB, b % NB
            keep = flag_ref[(m * SIDE * SIDE + s) * NB * NB + b]
            row = pl.multiple_of(jnp.minimum(rank, CAP - 1) * BLK, BLK)
            tile = packed[0, pl.ds(row, BLK), :]
            dense[i * BLK : (i + 1) * BLK, j * BLK : (j + 1) * BLK] = tile * keep.astype(F32).astype(BF16)
            rank = rank + keep
        w = t_ref.shape[2]
        acc[...] += jnp.dot(t_ref[0], dense[:w], preferred_element_type=F32) + jnp.dot(
            t_ref[1], dense[w:], preferred_element_type=F32
        )

    @pl.when(s == SIDE * SIDE - 1)
    def _():
        gate = ga[...]
        hidden = (gate / (1.0 + jnp.exp(-gate)) * ua[...]).astype(BF16)
        rows = hidden.shape[0] // 2

        @pl.when(at_ref[2] == 0)
        def _():
            own_ref[0, 0] = hidden[:rows]
            other_ref[...] = hidden[rows:]

        @pl.when(at_ref[2] == 1)
        def _():
            own_ref[0, 0] = hidden[rows:]
            other_ref[...] = hidden[:rows]


def make_hidden(flags, at, g, u, t):
    rows = t.shape[1]
    return pl.pallas_call(
        hidden_kernel,
        grid_spec=pltpu.PrefetchScalarGridSpec(
            num_scalar_prefetch=2,
            grid=(SIDE * SIDE,),
            in_specs=[
                pl.BlockSpec((1, PACK, BLK), lambda s, *_: (s, 0, 0)),
                pl.BlockSpec((1, PACK, BLK), lambda s, *_: (s, 0, 0)),
                pl.BlockSpec((2,) + t.shape[1:], lambda s, *_: (s, 0, 0)),
            ],
            out_specs=[
                pl.BlockSpec((1, 1, rows // 2, SHARD), lambda s, f, at: (at[2], at[0], 0, 0)),
                pl.BlockSpec((rows // 2, SHARD), lambda s, *_: (0, 0)),
            ],
            scratch_shapes=[
                pltpu.VMEM((SHARD, SHARD), BF16),
                pltpu.VMEM((SHARD, SHARD), BF16),
                pltpu.VMEM((rows, SHARD), F32),
                pltpu.VMEM((rows, SHARD), F32),
            ],
        ),
        out_shape=[
            jax.ShapeDtypeStruct((2, SIDE * SIDE, rows // 2, SHARD), BF16),
            jax.ShapeDtypeStruct((rows // 2, SHARD), BF16),
        ],
        name="make_hidden",
    )(flags, at, g, u, t)


def spread_kernel(h_in, o_ref, h, ass, ar, bs, br, ps, pr):
    del h_in
    x, y, z, c = place()
    other = device(x, y, z, 1 - c)
    greet(
        (
            device(wrap(x + 1, SIDE), y, z, c),
            device(wrap(x - 1, SIDE), y, z, c),
            device(x, wrap(y + 1, SIDE), z, c),
            device(x, wrap(y - 1, SIDE), z, c),
            other,
        )
    )
    me = y * SIDE + x
    swap = pltpu.make_async_remote_copy(
        src_ref=o_ref,
        dst_ref=h.at[c, me],
        send_sem=ps.at[0],
        recv_sem=pr.at[0],
        device_id=other,
        device_id_type=MESH,
    )
    swap.start()
    rows = h.shape[2]
    first, second = pl.ds(0, rows // 2), pl.ds(rows // 2, rows // 2)
    aa = halves(Gather(h.at[c], None, True, ass, ar), first, second)
    bb = halves(Gather(h.at[1 - c], None, False, bs, br), first, second)
    aa.first()
    aa.second(0)
    got = h.at[1 - c, me]
    pltpu.make_async_remote_copy(
        src_ref=got, dst_ref=got, send_sem=ps.at[0], recv_sem=pr.at[0], device_id=other, device_id_type=MESH
    ).wait_recv()
    bb.first()
    bb.second(0)
    aa.relay()
    aa.second(1)
    aa.second(2)
    bb.relay()
    bb.second(1)
    bb.second(2)
    aa.relay2(0)
    bb.relay2(0)
    aa.far()
    aa.second(3)
    bb.far()
    bb.second(3)
    for i in (1, 2, 3):
        aa.relay2(i)
        bb.relay2(i)
    for i in range(4):
        aa.far2(i)
        bb.far2(i)
    swap.wait_send()
    aa.drain()
    bb.drain()


def spread_hidden(h, other):
    dma = pltpu.SemaphoreType.DMA
    return pl.pallas_call(
        spread_kernel,
        out_shape=jax.ShapeDtypeStruct(h.shape, h.dtype),
        in_specs=[pl.BlockSpec(memory_space=HBM)] * 2,
        out_specs=pl.BlockSpec(memory_space=HBM),
        input_output_aliases={0: 0},
        scratch_shapes=[dma((20,))] * 4 + [dma((1,))] * 2,
        compiler_params=pltpu.CompilerParams(collective_id=1, has_side_effects=True),
        name="spread_hidden",
    )(h, other)


PARTS = 2


def reduce_kernel(h_ref, d_ref, o_ref, p, up_buf, down_buf, us, ur, ds, dr):
    x, y, z, c = place()
    up, down = device(x, y, wrap(z + 1, RING), c), device(x, y, wrap(z - 1, RING), c)
    greet((up, down))
    blocks, rows = h_ref.shape[1], h_ref.shape[2]
    group = 4

    @pl.loop(0, blocks // group)
    def _(i):
        at = pl.ds(i * group, group)
        width = h_ref.shape[3]
        own = h_ref[0, at].reshape(group * rows, width)
        far = h_ref[1, at].reshape(group * rows, width)
        sums = jnp.dot(own, d_ref[0], preferred_element_type=F32) + jnp.dot(
            far, d_ref[1], preferred_element_type=F32
        )
        p[at] = sums.reshape(group, rows, d_ref.shape[2])

    far_up, far_down = RING // 2, RING // 2 - 1
    piece = rows // PARTS

    def send(buf, step, q, dev, ss, rs, src):
        cp = pltpu.make_async_remote_copy(
            src_ref=src,
            dst_ref=buf.at[step, q],
            send_sem=ss.at[step * PARTS + q],
            recv_sem=rs.at[step * PARTS + q],
            device_id=dev,
            device_id_type=MESH,
        )
        return cp

    sends = []
    for q in range(PARTS):
        r = pl.ds(q * piece, piece)
        a = send(up_buf, 0, q, up, us, ur, p.at[wrap(z + far_up, RING), r])
        a.start()
        b = send(down_buf, 0, q, down, ds, dr, p.at[wrap(z - far_down, RING), r])
        b.start()
        sends += [a, b]
    for step in range(1, far_up + 1):
        for q in range(PARTS):
            r = pl.ds(q * piece, piece)
            send(up_buf, step - 1, q, up, us, ur, up_buf.at[step - 1, q]).wait_recv()
            if step < far_up:
                up_buf[step - 1, q] += p[wrap(z + far_up - step, RING), r]
                a = send(up_buf, step, q, up, us, ur, up_buf.at[step - 1, q])
                a.start()
                sends.append(a)
            if step <= far_down:
                send(down_buf, step - 1, q, down, ds, dr, down_buf.at[step - 1, q]).wait_recv()
                if step < far_down:
                    down_buf[step - 1, q] += p[wrap(z - far_down + step, RING), r]
                    b = send(down_buf, step, q, down, ds, dr, down_buf.at[step - 1, q])
                    b.start()
                    sends.append(b)
            if step == far_up:
                total = p[z, r] + up_buf[far_up - 1, q] + down_buf[far_down - 1, q]
                o_ref[r, :] = total.astype(BF16)
    for cp in sends:
        cp.wait_send()


def reduce_sums(h, d):
    dma = pltpu.SemaphoreType.DMA
    _, blocks, rows, _ = h.shape
    cols = d.shape[2]
    n_up, n_down = RING // 2, RING // 2 - 1
    return pl.pallas_call(
        reduce_kernel,
        out_shape=jax.ShapeDtypeStruct((rows, cols), BF16),
        in_specs=[pl.BlockSpec(memory_space=VMEM)] * 2,
        out_specs=pl.BlockSpec(memory_space=VMEM),
        scratch_shapes=[
            pltpu.VMEM((blocks, rows, cols), F32),
            pltpu.VMEM((n_up, PARTS, rows // PARTS, cols), F32),
            pltpu.VMEM((n_down, PARTS, rows // PARTS, cols), F32),
            dma((n_up * PARTS,)),
            dma((n_up * PARTS,)),
            dma((n_down * PARTS,)),
            dma((n_down * PARTS,)),
        ],
        compiler_params=pltpu.CompilerParams(collective_id=2, has_side_effects=True, vmem_limit_bytes=32 << 20),
        name="reduce_sums",
    )(h, d)


def local(tokens, gate_weight, up_weight, down_weight, gate_keep, up_keep, down_keep):
    t = lax.axis_index("tok")
    h = lax.axis_index("hid")
    at = jnp.stack([t, h, lax.rem(h, 2)]).astype(jnp.int32)
    g, u, x, d = pack(at, tokens, gate_weight, up_weight, down_weight, gate_keep, up_keep, down_keep)
    g, u, x, d = gather_weights(g, u, x, d)
    flags = jnp.stack([g[:, CAP * BLK, : NB * NB], u[:, CAP * BLK, : NB * NB]])
    flags = flags.astype(F32).astype(jnp.int32).reshape(-1)
    own, other = make_hidden(flags, at, g, u, x)
    hidden = spread_hidden(own, other)
    return reduce_sums(hidden, d)


def solution(mesh):
    return jax.shard_map(
        local,
        mesh=mesh,
        in_specs=(
            P("tok", "hid"),
            P("tok", "hid"),
            P("tok", "hid"),
            P("hid", "tok"),
            P("tok", "hid"),
            P("tok", "hid"),
            P("hid", "tok"),
        ),
        out_specs=P("hid", "tok"),
        check_vma=False,
    )
```

time: 434 us -> 141 us (0.32)
  waiting for transfers between devices: 335 us -> 0 us
  Pallas kernels: 0 us -> 135 us
  blocking collectives: 39.9 us -> 0 us
  matrix products: 24.9 us -> 0 us
  between operations: 13.3 us -> 0.05 us
  local copies, waits for them, and re-layouts: 16.4 us -> 4.43 us
    all_gather x4 -> x0, waiting for transfers between devices: 220 us -> none  [the longest x1 64.5 us: local(): features_all = lax.all_gather(tokens, 'hid', axis=1, tiled=True)]
    pallas_call x0 -> x5, Pallas kernels: none -> 135 us  [the longest x1 58 us: gather_weights(): pl.pallas_call(gather_kernel, out_shape=[jax.ShapeDtypeStruct(a.shape, a....]
    reduce_scatter x1 -> x0, waiting for transfers between devices: 115 us -> none  [local(): lax.psum_scatter(partial_sums, 'hid', scatter_dimension=0, tiled=True)]
    all_gather x2 -> x0, blocking collectives: 39.9 us -> none  [the longest x1 22.8 us: local(): lax.all_gather(gate_flags, 'tok', axis=0, tiled=True)]
    dot_general x7 -> x0, matrix products: 24.9 us -> none  [the longest x2 9.73 us: add_product(): jnp.dot(features_all, dense_strip, preferred_element_type=jnp.float32)]
    reshape x4 -> x0, local copies, waits for them, and re-layouts: 14.1 us -> none  [the longest x2 11.8 us: unpack_blocks(): dense_tiles.reshape(shards, block_rows, block_cols, side, side)]
  transfers between devices with their start and end apart: 5 -> 0, of which waited for: 5 -> 0; matrix products, arithmetic and copies ran while one was open for 5% -> 0% of each run, Pallas kernels for 0% -> 0%
where the time goes in v1:
time: 141 us; the launch traced here: 140 us
  Pallas kernels  135 us (96%)
  local copies, waits for them, and re-layouts  4.43 us (3%)
    pallas_call x1, Pallas kernels, gather_weights(): pl.pallas_call(gather_kernel, out_shape=[jax.ShapeDtypeStruct(a.shape, a....  58 us
    pallas_call x1, Pallas kernels, reduce_sums(): pl.pallas_call(reduce_kernel, out_shape=jax.ShapeDtypeStruct((rows, cols)...  36.9 us
    pallas_call x1, Pallas kernels, spread_hidden(): pl.pallas_call(spread_kernel, out_shape=jax.ShapeDtypeStruct(h.shape, h.d...  21.2 us
    pallas_call x1, Pallas kernels, make_hidden(): pl.pallas_call(hidden_kernel, grid_spec=pltpu.PrefetchScalarGridSpec(num_...  15 us
    pallas_call x1, Pallas kernels, pack(): pl.pallas_call(pack_kernel, grid_spec=pltpu.PrefetchScalarGridSpec(num_sc...  3.67 us

profile of v1, /device:TPU:6, one launch (start us, length us, event | category | flops | bytes accessed | tf_op | source)
XLA Modules:
  0.0 140.0 jit_solution(10963731787742093614)
XLA Ops:
  0.0 0.7 pad_add_fusion.at_ref
  0.7 3.7 %pack.1 = (bf16[16,1040,128]{2,1,0:T(8,128)(2,1)}, bf16[16,1040,128]{2,1,0:T(8,128)(2,1)}, bf16[32,128,256]{2,1,0:T(8,128)(2,1)}, bf16[2,512,512]{2,1,0:T(8,128)(2,1)}) custom-call(s32[3]{0:T(128)} %pad_add_fusion.at_ref, s32[4,4]{1,0:T(4,128)} %gk_ref.1, s32[4,4]{1,0:T(4,128)} %uk_ref.1, s32[4,4]{1,0:T(4,128)} %dk_ref.1, bf16[128,256]{1,0:T(8,128)(2,1)} %tok_ref.1, ...), custom_call_target="tpu_custom_call" | custom-call | tf_op jit(solution)/shard_map/pack/pallas_call | solution.py:170
  4.3 58.0 %gather_weights.1 = (bf16[16,1040,128]{2,1,0:T(8,128)(2,1)}, bf16[16,1040,128]{2,1,0:T(8,128)(2,1)}, bf16[32,128,256]{2,1,0:T(8,128)(2,1)}, bf16[2,512,512]{2,1,0:T(8,128)(2,1)}) custom-call(bf16[16,1040,128]{2,1,0:T(8,128)(2,1)} %get-tuple-element.15.g_in, ...), custom_call_target="tpu_custom_call", output_to_operand_aliasing={{0}: (0, {}), {1}: (1, {}), {2}: (2, {}), {3}: (3, {})} | custom-call | tf_op jit(solution)/shard_map/gather_weights/pallas_call | solution.py:305
  62.3 0.8 slice.6
  63.1 0.8 slice.7
  63.9 0.7 convert_element_type.14.flag_ref
  64.6 15.0 %make_hidden.1 = (bf16[2,16,64,512]{3,2,1,0:T(8,128)(2,1)}, bf16[64,512]{1,0:T(8,128)(2,1)}) custom-call(s32[512]{0:T(512)} %convert_element_type.14.flag_ref, s32[3]{0:T(128)} %pad_add_fusion.at_ref, bf16[16,1040,128]{2,1,0:T(8,128)(2,1)} %get-tuple-element.19.g_ref, bf16[16,1040,128]{2,1,0:T(8,128)(2,1)} %get-tuple-element.20.u_ref, ...), custom_call_target="tpu_custom_call" | custom-call | tf_op jit(solution)/shard_map/make_hidden/pallas_call | solution.py:358
  79.5 0.0 copy-start.1
  79.5 21.2 %spread_hidden.1.h_ref = bf16[2,16,64,512]{3,2,1,0:T(8,128)(2,1)} custom-call(bf16[2,16,64,512]{3,2,1,0:T(8,128)(2,1)} %get-tuple-element.22.h_in, bf16[64,512]{1,0:T(8,128)(2,1)} %get-tuple-element.23.o_ref), custom_call_target="tpu_custom_call", output_to_operand_aliasing={{}: (0, {})} | custom-call | tf_op jit(solution)/shard_map/spread_hidden/pallas_call | solution.py:447
  100.8 0.0 copy-done.1
  100.8 0.0 copy-start
  100.8 1.6 %copy-done = bf16[2,16,64,512]{3,2,1,0:T(8,128)(2,1)S(1)} copy-done((bf16[2,16,64,512]{3,2,1,0:T(8,128)(2,1)S(1)}, bf16[2,16,64,512]{3,2,1,0:T(8,128)(2,1)}, u32[]{:S(2)}) %copy-start) | copy-done | bytes 2097176
  102.4 36.9 %reduce_sums.1 = bf16[64,512]{1,0:T(8,128)(2,1)S(1)} custom-call(bf16[2,16,64,512]{3,2,1,0:T(8,128)(2,1)S(1)} %copy-done, bf16[2,512,512]{2,1,0:T(8,128)(2,1)S(1)} %copy-done.1), custom_call_target="tpu_custom_call" | custom-call | tf_op jit(solution)/shard_map/reduce_sums/pallas_call | solution.py:530
  139.3 0.6 copy.24
  (2 shorter events, 0.0 us)
Async XLA Ops:
  79.5 21.3 %copy-start.1 = (bf16[2,512,512]{2,1,0:T(8,128)(2,1)S(1)}, bf16[2,512,512]{2,1,0:T(8,128)(2,1)}, u32[]{:S(2)}) copy-start(bf16[2,512,512]{2,1,0:T(8,128)(2,1)} %get-tuple-element.24.d_ref) | copy-start | bytes 3145732
  100.8 1.6 %copy-start = (bf16[2,16,64,512]{3,2,1,0:T(8,128)(2,1)S(1)}, bf16[2,16,64,512]{3,2,1,0:T(8,128)(2,1)}, u32[]{:S(2)}) copy-start(bf16[2,16,64,512]{3,2,1,0:T(8,128)(2,1)} %spread_hidden.1.h_ref) | copy-start | bytes 6291460

commit v2 on v0

v2 whole, which is shorter than its diff:
```python
import functools

import jax
import jax.numpy as jnp
from jax import lax
from jax.experimental import pallas as pl
from jax.experimental.pallas import tpu as pltpu
from jax.sharding import PartitionSpec as P

MESH = pl.DeviceIdType.MESH
HBM = pltpu.MemorySpace.HBM
VMEM = pltpu.MemorySpace.VMEM
BF16 = jnp.bfloat16
F32 = jnp.float32

SIDE = 4
RING = 16
BLK = 128
NB = 4
CAP = 8
SHARD = NB * BLK
PACK = CAP * BLK


def place():
    t = lax.axis_index("tok")
    h = lax.axis_index("hid")
    return lax.rem(t, SIDE), lax.div(t, SIDE), lax.div(h, 2), lax.rem(h, 2)


def wrap(i, n):
    return lax.rem(i + n, n)


def device(x, y, z, c):
    return (y * SIDE + x, z * 2 + c)


def greet(peers):
    barrier = pltpu.get_barrier_semaphore()
    for peer in peers:
        pl.semaphore_signal(barrier, inc=1, device_id=peer, device_id_type=MESH)
    pl.semaphore_wait(barrier, len(peers))


class Gather:
    def __init__(self, buf, rows, x_first, send, recv):
        x, y, z, c = place()
        self.buf, self.send, self.recv = buf, send, recv
        self.split = rows > 1
        self.pieces = (pl.ds(0, rows // 2), pl.ds(rows // 2, rows // 2))
        self.a, self.b = (x, y) if x_first else (y, x)
        self.slot = lambda a, b: (b * SIDE + a) if x_first else (a * SIDE + b)
        self.dev = lambda a, b: device(a, b, z, c) if x_first else device(b, a, z, c)
        self.copies = {}

    def part(self, slot, piece):
        ref = self.buf.at[slot]
        if piece is None:
            return ref
        return ref.at[self.pieces[piece]]

    def copy(self, key, index, slot, piece, dev):
        ref = self.part(slot, piece)
        cp = pltpu.make_async_remote_copy(
            src_ref=ref,
            dst_ref=ref,
            send_sem=self.send.at[index],
            recv_sem=self.recv.at[index],
            device_id=dev,
            device_id_type=MESH,
        )
        cp.start()
        self.copies[key] = cp

    def got(self, index, slot, piece):
        ref = self.part(slot, piece)
        x, y, z, c = place()
        pltpu.make_async_remote_copy(
            src_ref=ref,
            dst_ref=ref,
            send_sem=self.send.at[index],
            recv_sem=self.recv.at[index],
            device_id=self.dev(wrap(self.a + 1, SIDE), self.b),
            device_id_type=MESH,
        ).wait_recv()

    def first(self):
        s = self.slot(self.a, self.b)
        self.copy("r", 0, s, None, self.dev(wrap(self.a + 1, SIDE), self.b))
        self.copy("l", 1, s, None, self.dev(wrap(self.a - 1, SIDE), self.b))

    def relay(self):
        left = self.slot(wrap(self.a - 1, SIDE), self.b)
        right = self.slot(wrap(self.a + 1, SIDE), self.b)
        self.got(0, left, None)
        self.copy("fr", 2, left, 0 if self.split else None, self.dev(wrap(self.a + 1, SIDE), self.b))
        self.got(1, right, None)
        if self.split:
            self.copy("fl", 3, right, 1, self.dev(wrap(self.a - 1, SIDE), self.b))

    def far(self):
        opposite = self.slot(wrap(self.a + 2, SIDE), self.b)
        self.got(2, opposite, 0 if self.split else None)
        if self.split:
            self.got(3, opposite, 1)

    OFF = (0, -1, 1, 2)

    def second(self, i):
        a = wrap(self.a + self.OFF[i], SIDE)
        s = self.slot(a, self.b)
        self.copy(("u", i), 4 + 4 * i, s, None, self.dev(self.a, wrap(self.b + 1, SIDE)))
        self.copy(("d", i), 5 + 4 * i, s, None, self.dev(self.a, wrap(self.b - 1, SIDE)))

    def relay2(self, i):
        a = wrap(self.a + self.OFF[i], SIDE)
        below = self.slot(a, wrap(self.b - 1, SIDE))
        above = self.slot(a, wrap(self.b + 1, SIDE))
        self.got(4 + 4 * i, below, None)
        self.copy(("fu", i), 6 + 4 * i, below, 0 if self.split else None, self.dev(self.a, wrap(self.b + 1, SIDE)))
        self.got(5 + 4 * i, above, None)
        if self.split:
            self.copy(("fd", i), 7 + 4 * i, above, 1, self.dev(self.a, wrap(self.b - 1, SIDE)))

    def far2(self, i):
        a = wrap(self.a + self.OFF[i], SIDE)
        s = self.slot(a, wrap(self.b + 2, SIDE))
        self.got(6 + 4 * i, s, 0 if self.split else None)
        if self.split:
            self.got(7 + 4 * i, s, 1)

    def drain(self):
        for cp in self.copies.values():
            cp.wait_send()


def pack_kernel(gk_ref, uk_ref, dk_ref, gw_ref, uw_ref, dw_ref, m_ref, g_ref, u_ref, d_ref):
    lane = lax.broadcasted_iota(jnp.int32, m_ref.shape, 1)
    flags = jnp.zeros(m_ref.shape, jnp.int32)
    for m, (keep_ref, w_ref, o_ref) in enumerate(((gk_ref, gw_ref, g_ref), (uk_ref, uw_ref, u_ref))):
        o_ref[...] = jnp.zeros_like(o_ref)
        rank = jnp.int32(0)
        for b in range(NB * NB):
            i, j = b // NB, b % NB
            keep = keep_ref[i, j]

            @pl.when(keep == 1)
            def _(i=i, j=j, rank=rank, w_ref=w_ref, o_ref=o_ref):
                row = pl.multiple_of(jnp.minimum(rank, CAP - 1) * BLK, BLK)
                o_ref[pl.ds(row, BLK), :] = w_ref[i * BLK : (i + 1) * BLK, j * BLK : (j + 1) * BLK]

            flags = jnp.where(lane == m * NB * NB + b, keep, flags)
            rank = rank + keep
    m_ref[...] = flags
    for i in range(NB):
        for j in range(NB):
            r, s = slice(i * BLK, (i + 1) * BLK), slice(j * BLK, (j + 1) * BLK)
            d_ref[r, s] = dw_ref[r, s] * dk_ref[i, j].astype(F32).astype(BF16)


def pack(gw, uw, dw, gk, uk, dk):
    return pl.pallas_call(
        pack_kernel,
        in_specs=[pl.BlockSpec(memory_space=pltpu.MemorySpace.SMEM)] * 3 + [pl.BlockSpec(memory_space=VMEM)] * 3,
        out_specs=[pl.BlockSpec(memory_space=VMEM)] * 4,
        out_shape=[
            jax.ShapeDtypeStruct((1, BLK), jnp.int32),
            jax.ShapeDtypeStruct((PACK, BLK), BF16),
            jax.ShapeDtypeStruct((PACK, BLK), BF16),
            jax.ShapeDtypeStruct(dw.shape, BF16),
        ],
        name="pack",
    )(gk, uk, dk, gw, uw, dw)


def remote(src, dst, send, recv, dev):
    return pltpu.make_async_remote_copy(
        src_ref=src, dst_ref=dst, send_sem=send, recv_sem=recv, device_id=dev, device_id_type=MESH
    )


def hidden_kernel(
    m_in, g_in, u_in, t_in, d_in, hid, far_d, m, g, u, t, gp, up_, gd, ud, ga, ua, flags,
    gs, gr, us, ur, ms, mr, zs, zr, cs, cr, ds, dr, ls,
):
    x, y, z, c = place()
    me, h = y * SIDE + x, z * 2 + c
    up, down = device(x, y, wrap(z + 1, RING), c), device(x, y, wrap(z - 1, RING), c)
    other = device(x, y, z, 1 - c)
    own = [
        pltpu.make_async_copy(src, dst, ls.at[i])
        for i, (src, dst) in enumerate(((t_in, t.at[h]), (g_in, g.at[me]), (u_in, u.at[me]), (m_in, m.at[me])))
    ]
    for cp in own:
        cp.start()
    greet(
        (
            device(wrap(x + 1, SIDE), y, z, c),
            device(wrap(x - 1, SIDE), y, z, c),
            device(x, wrap(y + 1, SIDE), z, c),
            device(x, wrap(y - 1, SIDE), z, c),
            up,
            down,
            other,
        )
    )
    for cp in own:
        cp.wait()
    gg = Gather(g, PACK, True, gs, gr)
    uu = Gather(u, PACK, False, us, ur)
    mm = Gather(m, 1, True, ms, mr)
    sends = []

    def z_copy(block, dev, send, recv, start):
        ref = t.at[2 * block + c]
        cp = remote(ref, ref, send, recv, dev)
        if start:
            cp.start()
            sends.append(cp)
        else:
            cp.wait_recv()

    def z_step(k):
        z_copy(wrap(z - (k - 1), RING), up, zs.at[2 * k - 2], zr.at[2 * k - 2], True)
        if k < RING // 2:
            z_copy(wrap(z + (k - 1), RING), down, zs.at[2 * k - 1], zr.at[2 * k - 1], True)

    def z_wait(k):
        z_copy(wrap(z - k, RING), up, zs.at[2 * k - 2], zr.at[2 * k - 2], False)
        if k < RING // 2:
            z_copy(wrap(z + k, RING), down, zs.at[2 * k - 1], zr.at[2 * k - 1], False)

    def z_share(k):
        z_copy(wrap(z - k, RING), other, cs.at[2 * k - 1], cr.at[2 * k - 1], True)
        if k < RING // 2:
            z_copy(wrap(z + k, RING), other, cs.at[2 * k], cr.at[2 * k], True)

    def z_go(k):
        z_wait(k)
        if k < RING // 2:
            z_step(k + 1)
        z_share(k)

    z_step(1)
    mm.first()
    mm.second(0)
    gg.first()
    uu.first()
    gg.second(0)
    uu.second(0)
    z_copy(z, other, cs.at[0], cr.at[0], True)
    d_copy = remote(d_in, far_d, ds.at[0], dr.at[0], other)
    d_copy.start()
    mm.relay()
    mm.second(1)
    mm.second(2)
    z_go(1)
    mm.relay2(0)
    mm.far()
    mm.second(3)
    z_go(2)
    gg.relay()
    uu.relay()
    gg.second(1)
    uu.second(1)
    gg.second(2)
    uu.second(2)
    for i in (1, 2, 3):
        mm.relay2(i)
    z_go(3)
    gg.relay2(0)
    uu.relay2(0)
    z_go(4)
    gg.far()
    uu.far()
    gg.second(3)
    uu.second(3)
    for i in range(4):
        mm.far2(i)
    z_go(5)
    gg.relay2(1)
    uu.relay2(1)
    z_go(6)
    gg.relay2(2)
    uu.relay2(2)
    flag_copy = pltpu.make_async_copy(m, flags, ls.at[4])
    flag_copy.start()
    ga[...] = jnp.zeros_like(ga)
    ua[...] = jnp.zeros_like(ua)
    z_go(7)
    z_go(8)
    for n in range(RING):
        k = (n + 1) // 2
        block = z if n == 0 else (wrap(z - k, RING) if n % 2 else wrap(z + k, RING))
        ref = t.at[2 * block + 1 - c]
        remote(ref, ref, cs.at[n], cr.at[n], other).wait_recv()
    flag_copy.wait()

    def shard(dx, dy):
        s = wrap(y + dy, SIDE) * SIDE + wrap(x + dx, SIDE)
        w = t.shape[2]
        for k, (buf, stage, dense, acc) in enumerate(((g, gp, gd, ga), (u, up_, ud, ua))):
            stage[...] = buf[s].reshape(stage.shape)
            rank = jnp.int32(0)
            for b in range(NB * NB):
                i, j = b // NB, b % NB
                keep = flags[s, 0, k * NB * NB + b]
                tile = stage[jnp.minimum(rank, CAP - 1)]
                dense[i * BLK : (i + 1) * BLK, j * BLK : (j + 1) * BLK] = tile * keep.astype(F32).astype(BF16)
                rank = rank + keep
            acc[...] += jnp.dot(t[2 * s], dense[:w], preferred_element_type=F32) + jnp.dot(
                t[2 * s + 1], dense[w:], preferred_element_type=F32
            )

    @pl.loop(0, 5)
    def _(n):
        sign = (1 - 2 * lax.rem(n + 1, 2)) * lax.div(n + 3, 4)
        on_x = 1 - lax.div(n, 3)
        shard(sign * on_x, sign * (1 - on_x))

    gg.relay2(3)
    uu.relay2(3)

    @pl.loop(0, 4)
    def _(n):
        shard(1 - 2 * lax.rem(n, 2), 1 - 2 * lax.div(n, 2))

    gg.far2(0)
    uu.far2(0)

    @pl.loop(0, 2)
    def _(n):
        shard(2 * n, 2 * (1 - n))

    for i in (1, 2):
        gg.far2(i)
        uu.far2(i)

    @pl.loop(0, 4)
    def _(n):
        sign = 1 - 2 * lax.rem(n, 2)
        on_x = lax.div(n, 2)
        shard(2 * on_x + sign * (1 - on_x), sign * on_x + 2 * (1 - on_x))

    gg.far2(3)
    uu.far2(3)
    shard(2, 2)
    gate = ga[...]
    hidden = (gate / (1.0 + jnp.exp(-gate)) * ua[...]).astype(BF16)
    hid[...] = hidden.reshape(hid.shape)
    remote(d_in, far_d, ds.at[0], dr.at[0], other).wait_recv()
    d_copy.wait_send()
    mm.drain()
    gg.drain()
    uu.drain()
    for cp in sends:
        cp.wait_send()


def make_hidden(m, g, u, t, d):
    dma = pltpu.SemaphoreType.DMA
    rows, width = t.shape
    chips = SIDE * SIDE
    hid, far_d, _ = pl.pallas_call(
        hidden_kernel,
        out_shape=[
            jax.ShapeDtypeStruct((2, rows // 2, SHARD), BF16),
            jax.ShapeDtypeStruct(d.shape, BF16),
            jax.ShapeDtypeStruct((chips,) + m.shape, m.dtype),
        ],
        in_specs=[pl.BlockSpec(memory_space=HBM)] * 5,
        out_specs=[
            pl.BlockSpec(memory_space=VMEM),
            pl.BlockSpec(memory_space=HBM),
            pl.BlockSpec(memory_space=HBM),
        ],
        scratch_shapes=[
            pltpu.VMEM((chips, PACK, BLK), BF16),
            pltpu.VMEM((chips, PACK, BLK), BF16),
            pltpu.VMEM((2 * RING, rows, width), BF16),
            pltpu.VMEM((CAP, BLK, BLK), BF16),
            pltpu.VMEM((CAP, BLK, BLK), BF16),
            pltpu.VMEM((SHARD, SHARD), BF16),
            pltpu.VMEM((SHARD, SHARD), BF16),
            pltpu.VMEM((rows, SHARD), F32),
            pltpu.VMEM((rows, SHARD), F32),
            pltpu.SMEM((chips,) + m.shape, jnp.int32),
        ]
        + [dma((20,))] * 6
        + [dma((15,))] * 2
        + [dma((16,))] * 2
        + [dma((1,))] * 2
        + [dma((5,))],
        compiler_params=pltpu.CompilerParams(collective_id=0, has_side_effects=True, vmem_limit_bytes=48 << 20),
        name="make_hidden",
    )(m, g, u, t, d)
    return hid, far_d


PARTS = 2


def tail_kernel(
    hid, d_own, d_far, o_ref, ha, hb, p, up_buf, down_buf,
    as0, ar0, as1, ar1, bs0, br0, bs1, br1, ps, pr, us, ur, ds, dr, ls,
):
    x, y, z, c = place()
    up, down = device(x, y, wrap(z + 1, RING), c), device(x, y, wrap(z - 1, RING), c)
    other = device(x, y, z, 1 - c)
    me = y * SIDE + x
    piece = ha.shape[2]
    own = [
        pltpu.make_async_copy(hid.at[c, pl.ds(q * piece, piece)], ha.at[q, me], ls.at[q]) for q in range(PARTS)
    ]
    for cp in own:
        cp.start()
    greet(
        (
            device(wrap(x + 1, SIDE), y, z, c),
            device(wrap(x - 1, SIDE), y, z, c),
            device(x, wrap(y + 1, SIDE), z, c),
            device(x, wrap(y - 1, SIDE), z, c),
            up,
            down,
            other,
        )
    )
    swaps = [
        remote(hid.at[1 - c, pl.ds(q * piece, piece)], hb.at[q, me], ps.at[q], pr.at[q], other) for q in range(PARTS)
    ]
    for cp in swaps:
        cp.start()
    for cp in own:
        cp.wait()
    a = [Gather(ha.at[q], piece, True, s, r) for q, (s, r) in enumerate(((as0, ar0), (as1, ar1)))]
    b = [Gather(hb.at[q], piece, False, s, r) for q, (s, r) in enumerate(((bs0, br0), (bs1, br1)))]
    sends = []
    far_up, far_down = RING // 2, RING // 2 - 1

    def begin(q):
        a[q].first()
        a[q].second(0)
        swaps[q].wait_recv()
        b[q].first()
        b[q].second(0)

    def near(q):
        for s in (a[q], b[q]):
            s.relay()
            s.second(1)
            s.second(2)

    def middle(q):
        for s in (a[q], b[q]):
            s.relay2(0)
        for s in (a[q], b[q]):
            s.far()
            s.second(3)

    def late(q):
        for i in (1, 2, 3):
            for s in (a[q], b[q]):
                s.relay2(i)

    def end(q):
        for i in range(4):
            for s in (a[q], b[q]):
                s.far2(i)

    def multiply(q):
        blocks, _, width = ha.shape[1:]
        left = ha[q].reshape(blocks * piece, width)
        right = hb[q].reshape(blocks * piece, width)
        sums = jnp.dot(left, d_own[...], preferred_element_type=F32) + jnp.dot(
            right, d_far[...], preferred_element_type=F32
        )
        p[q] = sums.reshape(p.shape[1:])

    def ring(buf, step, q, dev, ss, rs, src):
        n = step * PARTS + q
        return remote(src, buf.at[step, q], ss.at[n], rs.at[n], dev)

    def push(q):
        for buf, dev, ss, rs, block in (
            (up_buf, up, us, ur, wrap(z + far_up, RING)),
            (down_buf, down, ds, dr, wrap(z - far_down, RING)),
        ):
            cp = ring(buf, 0, q, dev, ss, rs, p.at[q, block])
            cp.start()
            sends.append(cp)

    def step(k, q):
        for buf, dev, ss, rs, far, block in (
            (up_buf, up, us, ur, far_up, wrap(z + far_up - k, RING)),
            (down_buf, down, ds, dr, far_down, wrap(z - far_down + k, RING)),
        ):
            if k > far:
                continue
            here = buf.at[k - 1, q]
            ring(buf, k - 1, q, dev, ss, rs, here).wait_recv()
            if k < far:
                buf[k - 1, q] += p[q, block]
                cp = ring(buf, k, q, dev, ss, rs, here)
                cp.start()
                sends.append(cp)
        if k == far_up:
            total = p[q, z] + up_buf[far_up - 1, q] + down_buf[far_down - 1, q]
            o_ref[q * piece : (q + 1) * piece, :] = total.astype(BF16)

    begin(0)
    near(0)
    begin(1)
    middle(0)
    near(1)
    late(0)
    middle(1)
    end(0)
    multiply(0)
    push(0)
    late(1)
    step(1, 0)
    end(1)
    multiply(1)
    push(1)
    for k in range(2, far_up + 1):
        step(k, 0)
        step(k - 1, 1)
    step(far_up, 1)
    for cp in swaps:
        cp.wait_send()
    for s in a + b:
        s.drain()
    for cp in sends:
        cp.wait_send()


def tail(hid, d_own, d_far):
    dma = pltpu.SemaphoreType.DMA
    _, rows, width = hid.shape
    cols = d_own.shape[1]
    chips = SIDE * SIDE
    n_up, n_down = RING // 2, RING // 2 - 1
    piece = rows // PARTS
    return pl.pallas_call(
        tail_kernel,
        out_shape=jax.ShapeDtypeStruct((rows, cols), BF16),
        in_specs=[pl.BlockSpec(memory_space=HBM)] + [pl.BlockSpec(memory_space=VMEM)] * 2,
        out_specs=pl.BlockSpec(memory_space=VMEM),
        scratch_shapes=[
            pltpu.VMEM((PARTS, chips, piece, width), BF16),
            pltpu.VMEM((PARTS, chips, piece, width), BF16),
            pltpu.VMEM((PARTS, chips, piece, cols), F32),
            pltpu.VMEM((n_up, PARTS, piece, cols), F32),
            pltpu.VMEM((n_down, PARTS, piece, cols), F32),
        ]
        + [dma((20,))] * 8
        + [dma((PARTS,))] * 2
        + [dma((n_up * PARTS,))] * 2
        + [dma((n_down * PARTS,))] * 2
        + [dma((PARTS,))],
        compiler_params=pltpu.CompilerParams(collective_id=1, has_side_effects=True, vmem_limit_bytes=48 << 20),
        name="tail",
    )(hid, d_own, d_far)


def local(tokens, gate_weight, up_weight, down_weight, gate_keep, up_keep, down_keep):
    m, g, u, d = pack(gate_weight, up_weight, down_weight, gate_keep, up_keep, down_keep)
    hid, far_d = make_hidden(m, g, u, tokens, d)
    return tail(hid, d, far_d)


def solution(mesh):
    return jax.shard_map(
        local,
        mesh=mesh,
        in_specs=(
            P("tok", "hid"),
            P("tok", "hid"),
            P("tok", "hid"),
            P("hid", "tok"),
            P("tok", "hid"),
            P("tok", "hid"),
            P("hid", "tok"),
        ),
        out_specs=P("hid", "tok"),
        check_vma=False,
    )
```

time: 434 us -> 128 us (0.29)
  waiting for transfers between devices: 335 us -> 0 us
  Pallas kernels: 0 us -> 124 us
  blocking collectives: 39.9 us -> 0 us
  matrix products: 24.9 us -> 0 us
  between operations: 13.3 us -> 0.03 us
  local copies, waits for them, and re-layouts: 16.4 us -> 4.23 us
    all_gather x4 -> x0, waiting for transfers between devices: 220 us -> none  [the longest x1 64.5 us: local(): features_all = lax.all_gather(tokens, 'hid', axis=1, tiled=True)]
    pallas_call x0 -> x3, Pallas kernels: none -> 124 us  [the longest x1 64.5 us: make_hidden(): pl.pallas_call(hidden_kernel, out_shape=[jax.ShapeDtypeStruct((2, rows //...]
    reduce_scatter x1 -> x0, waiting for transfers between devices: 115 us -> none  [local(): lax.psum_scatter(partial_sums, 'hid', scatter_dimension=0, tiled=True)]
    all_gather x2 -> x0, blocking collectives: 39.9 us -> none  [the longest x1 22.8 us: local(): lax.all_gather(gate_flags, 'tok', axis=0, tiled=True)]
    dot_general x7 -> x0, matrix products: 24.9 us -> none  [the longest x2 9.73 us: add_product(): jnp.dot(features_all, dense_strip, preferred_element_type=jnp.float32)]
    reshape x4 -> x0, local copies, waits for them, and re-layouts: 14.1 us -> none  [the longest x2 11.8 us: unpack_blocks(): dense_tiles.reshape(shards, block_rows, block_cols, side, side)]
  transfers between devices with their start and end apart: 5 -> 0, of which waited for: 5 -> 0; matrix products, arithmetic and copies ran while one was open for 5% -> 0% of each run, Pallas kernels for 0% -> 0%
where the time goes in v2:
time: 128 us
  Pallas kernels  124 us (97%)
  local copies, waits for them, and re-layouts  4.23 us (3%)
    pallas_call x1, Pallas kernels, make_hidden(): pl.pallas_call(hidden_kernel, out_shape=[jax.ShapeDtypeStruct((2, rows //...  64.5 us
    pallas_call x1, Pallas kernels, tail(): pl.pallas_call(tail_kernel, out_shape=jax.ShapeDtypeStruct((rows, cols),...  56.6 us
    unnamed x13, local copies, waits for them, and re-layouts  4.23 us
    pallas_call x1, Pallas kernels, pack(): pl.pallas_call(pack_kernel, in_specs=[pl.BlockSpec(memory_space=pltpu.Mem...  2.86 us

profile of v2, /device:TPU:6, one launch (start us, length us, event | category | flops | bytes accessed | tf_op | source)
XLA Modules:
  0.0 128.2 jit_solution(3791641209440427415)
XLA Ops:
  0.0 0.0 copy-start.4
  0.0 2.9 %pack.1 = (s32[1,128]{1,0:T(1,128)}, bf16[1024,128]{1,0:T(8,128)(2,1)}, bf16[1024,128]{1,0:T(8,128)(2,1)}, bf16[512,512]{1,0:T(8,128)(2,1)}) custom-call(s32[4,4]{1,0:T(4,128)} %gk_ref.1, s32[4,4]{1,0:T(4,128)} %uk_ref.1, s32[4,4]{1,0:T(4,128)} %dk_ref.1, bf16[512,512]{1,0:T(8,128)(2,1)} %gw_ref.1, bf16[512,512]{1,0:T(8,128)(2,1)} %uw_ref.1, ...), custom_call_target="tpu_custom_call" | custom-call | tf_op jit(solution)/shard_map/pack/pallas_call | solution.py:163
  2.9 0.0 copy-start.5
  2.9 0.0 copy-done.4
  2.9 0.7 copy-done.5
  3.5 0.0 copy-start
  3.5 1.0 copy-done
  4.6 0.0 copy-start.2
  4.6 0.9 copy-done.2
  5.5 0.0 copy-start.3
  5.5 0.9 copy-done.3
  6.5 0.0 copy-start.1
  6.5 64.5 %make_hidden.1 = (bf16[2,64,512]{2,1,0:T(8,128)(2,1)S(1)}, bf16[512,512]{1,0:T(8,128)(2,1)S(1)}, s32[16,1,128]{2,1,0:T(1,128)}) custom-call(s32[1,128]{1,0:T(1,128)S(1)} %copy-done.5, bf16[1024,128]{1,0:T(8,128)(2,1)S(1)} %copy-done.2, bf16[1024,128]{1,0:T(8,128)(2,1)S(1)} %copy-done.3, bf16[128,256]{1,0:T(8,128)(2,1)S(1)} %copy-done.4, ...), custom_call_target="tpu_custom_call" | custom-call | tf_op jit(solution)/shard_map/make_hidden/pallas_call | solution.py:365
  70.9 0.0 copy-done.1
  70.9 56.6 %tail.1 = bf16[64,512]{1,0:T(8,128)(2,1)S(1)} custom-call(bf16[2,64,512]{2,1,0:T(8,128)(2,1)S(1)} %get-tuple-element.15.hid, bf16[512,512]{1,0:T(8,128)(2,1)S(1)} %copy-done.1, bf16[512,512]{1,0:T(8,128)(2,1)S(1)} %get-tuple-element.16.d_far), custom_call_target="tpu_custom_call" | custom-call | tf_op jit(solution)/shard_map/tail/pallas_call | solution.py:545
  127.5 0.6 copy.9
Async XLA Ops:
  0.0 2.9 %copy-start.4 = (bf16[128,256]{1,0:T(8,128)(2,1)S(1)}, bf16[128,256]{1,0:T(8,128)(2,1)}, u32[]{:S(2)}) copy-start(bf16[128,256]{1,0:T(8,128)(2,1)} %t_in.1) | copy-start | bytes 196612
  2.9 0.7 copy-start.5
  3.5 1.0 copy-start
  4.6 0.9 copy-start.2
  5.5 0.9 copy-start.3
  6.5 64.5 %copy-start.1 = (bf16[512,512]{1,0:T(8,128)(2,1)S(1)}, bf16[512,512]{1,0:T(8,128)(2,1)}, u32[]{:S(2)}) copy-start(bf16[512,512]{1,0:T(8,128)(2,1)} %get-tuple-element.14.d_in.d_own) | copy-start | bytes 1572868

commit v3 on v2

--- a/solution.py
+++ b/solution.py
@@ -180,180 +180,235 @@
     )
 
 
-def hidden_kernel(
-    m_in, g_in, u_in, t_in, d_in, hid, far_d, m, g, u, t, gp, up_, gd, ud, ga, ua, flags,
-    gs, gr, us, ur, ms, mr, zs, zr, cs, cr, ds, dr, ls,
-):
+class Line(Gather):
+    def __init__(self, buf, rows, along_x, send, recv):
+        super().__init__(buf, rows, along_x, send, recv)
+        self.slot = lambda a, b: a
+
+
+class Product:
+    def __init__(self, split_x, refs):
+        x, y, z, c = place()
+        self.a, self.b = (x, y) if split_x else (y, x)
+        self.dev = lambda a: device(a, y, z, c) if split_x else device(x, a, z, c)
+        self.part = (lambda s: (lax.rem(s, SIDE), lax.div(s, SIDE))) if split_x else (
+            lambda s: (lax.div(s, SIDE), lax.rem(s, SIDE))
+        )
+        (self.w, self.m, self.t, self.acc, self.far_in, self.near_in, self.flags) = refs[:7]
+        ws, wr, ms, mr, self.ts, self.tr, self.tl, self.hs, self.hr, self.rs, self.rr = refs[7:]
+        self.lane = 0 if split_x else NB * NB
+        self.weights = Line(self.w, PACK, not split_x, ws, wr)
+        self.masks = Line(self.m, 1, not split_x, ms, mr)
+
+    def block(self, j):
+        return self.t.at[j, place()[3], self.a]
+
+    def dispatch(self, src, s):
+        to, j = self.part(s)
+        off = wrap(to - self.a, SIDE)
+
+        @pl.when(off == 0)
+        def _():
+            pltpu.make_async_copy(src, self.block(j), self.tl.at[j]).start()
+
+        @pl.when(off != 0)
+        def _():
+            remote(src, self.block(j), self.ts.at[j, off], self.tr.at[j, off], self.dev(to)).start()
+
+    def collect(self, s, other):
+        to, j = self.part(s)
+
+        @pl.when(to == self.a)
+        def _():
+            ref = self.block(j)
+            pltpu.make_async_copy(ref, ref, self.tl.at[j]).wait()
+            for off in range(1, SIDE):
+                remote(ref, ref, self.ts.at[j, off], self.tr.at[j, off], other).wait_recv()
+            half = self.t.at[j, place()[3]]
+            remote(half, half, self.hs.at[j], self.hr.at[j], other).start()
+
+    def multiply(self, j, other, stage, dense):
+        half = self.t.at[j, 1 - place()[3]]
+        remote(half, half, self.hs.at[j], self.hr.at[j], other).wait_recv()
+        stage[...] = self.w[j].reshape(stage.shape)
+        rank = jnp.int32(0)
+        for n in range(NB * NB):
+            r, q = n // NB, n % NB
+            keep = self.flags[j, 0, self.lane + n]
+            tile = stage[jnp.minimum(rank, CAP - 1)]
+            dense[r * BLK : (r + 1) * BLK, q * BLK : (q + 1) * BLK] = tile * keep.astype(F32).astype(BF16)
+            rank = rank + keep
+        _, _, lines, rows, width = self.t.shape
+        left, right = self.t[j, 0].reshape(lines * rows, width), self.t[j, 1].reshape(lines * rows, width)
+        self.acc[...] += (
+            jnp.dot(left, dense[:width], preferred_element_type=F32)
+            + jnp.dot(right, dense[width:], preferred_element_type=F32)
+        ).reshape(self.acc.shape)
+
+    def sum_copy(self, n):
+        a, rows = self.a, self.acc.shape[1] // 2
+        right, left, far = wrap(a + 1, SIDE), wrap(a - 1, SIDE), wrap(a + 2, SIDE)
+        top, low = pl.ds(0, rows), pl.ds(rows, rows)
+        src, dst, to = (
+            (self.acc.at[far, top], self.far_in.at[0], right),
+            (self.acc.at[far, low], self.far_in.at[1], left),
+            (self.acc.at[right, low], self.near_in.at[0], right),
+            (self.acc.at[left, top], self.near_in.at[1], left),
+            (self.acc.at[right, top], self.near_in.at[2], right),
+            (self.acc.at[left, low], self.near_in.at[3], left),
+        )[n]
+        return remote(src, dst, self.rs.at[n], self.rr.at[n], self.dev(to))
+
+    def sum_start(self):
+        for n in range(4):
+            self.sum_copy(n).start()
+
+    def sum_relay(self):
+        a, rows = self.a, self.acc.shape[1] // 2
+        self.sum_copy(0).wait_recv()
+        self.acc[wrap(a + 1, SIDE), :rows] += self.far_in[0]
+        self.sum_copy(4).start()
+        self.sum_copy(1).wait_recv()
+        self.acc[wrap(a - 1, SIDE), rows:] += self.far_in[1]
+        self.sum_copy(5).start()
+
+    def total(self):
+        rows = self.acc.shape[1] // 2
+        for n in range(2, 6):
+            self.sum_copy(n).wait_recv()
+        top = self.acc[self.a, :rows] + self.near_in[1] + self.near_in[2]
+        low = self.acc[self.a, rows:] + self.near_in[0] + self.near_in[3]
+        return top, low
+
+    def drain(self, other):
+        for j in range(SIDE):
+            ref = self.block(j)
+            for off in range(1, SIDE):
+                remote(ref, ref, self.ts.at[j, off], self.tr.at[j, off], other).wait_send()
+            half = self.t.at[j, place()[3]]
+            remote(half, half, self.hs.at[j], self.hr.at[j], other).wait_send()
+        for n in range(6):
+            self.sum_copy(n).wait_send()
+        self.weights.drain()
+        self.masks.drain()
+
+
+def hidden_kernel(m_in, g_in, u_in, t_in, d_in, hid, far_d, mg, mu, ring, stage, dense, *refs):
     x, y, z, c = place()
-    me, h = y * SIDE + x, z * 2 + c
+    zs, zr, ds, dr, ls = refs[-5:]
+    per = len(refs[:-5]) // 2
+    g_refs, u_refs = refs[:per], refs[per : 2 * per]
+    gate = Product(True, (g_refs[0], mg) + g_refs[1:])
+    up_ = Product(False, (u_refs[0], mu) + u_refs[1:])
     up, down = device(x, y, wrap(z + 1, RING), c), device(x, y, wrap(z - 1, RING), c)
     other = device(x, y, z, 1 - c)
     own = [
         pltpu.make_async_copy(src, dst, ls.at[i])
-        for i, (src, dst) in enumerate(((t_in, t.at[h]), (g_in, g.at[me]), (u_in, u.at[me]), (m_in, m.at[me])))
+        for i, (src, dst) in enumerate(
+            (
+                (t_in, ring.at[z]),
+                (g_in, gate.w.at[y]),
+                (u_in, up_.w.at[x]),
+                (m_in, gate.m.at[y]),
+                (m_in, up_.m.at[x]),
+            )
+        )
     ]
     for cp in own:
         cp.start()
     greet(
-        (
-            device(wrap(x + 1, SIDE), y, z, c),
-            device(wrap(x - 1, SIDE), y, z, c),
-            device(x, wrap(y + 1, SIDE), z, c),
-            device(x, wrap(y - 1, SIDE), z, c),
-            up,
-            down,
-            other,
-        )
+        [device(wrap(x + k, SIDE), y, z, c) for k in (1, 2, 3)]
+        + [device(x, wrap(y + k, SIDE), z, c) for k in (1, 2, 3)]
+        + [up, down, other]
     )
     for cp in own:
         cp.wait()
-    gg = Gather(g, PACK, True, gs, gr)
-    uu = Gather(u, PACK, False, us, ur)
-    mm = Gather(m, 1, True, ms, mr)
     sends = []
-
-    def z_copy(block, dev, send, recv, start):
-        ref = t.at[2 * block + c]
-        cp = remote(ref, ref, send, recv, dev)
-        if start:
+    both = (gate, up_)
+
+    def z_copy(block, dev, send, recv):
+        return remote(ring.at[block], ring.at[block], send, recv, dev)
+
+    def z_step(k):
+        cp = z_copy(wrap(z - (k - 1), RING), up, zs.at[2 * k - 2], zr.at[2 * k - 2])
+        cp.start()
+        sends.append(cp)
+        if k < RING // 2:
+            cp = z_copy(wrap(z + (k - 1), RING), down, zs.at[2 * k - 1], zr.at[2 * k - 1])
             cp.start()
             sends.append(cp)
-        else:
-            cp.wait_recv()
-
-    def z_step(k):
-        z_copy(wrap(z - (k - 1), RING), up, zs.at[2 * k - 2], zr.at[2 * k - 2], True)
+
+    def blocks(k):
+        return (wrap(z - k, RING), wrap(z + k, RING))[: 1 if k in (0, RING // 2) else 2]
+
+    def z_go(k):
+        z_copy(wrap(z - k, RING), up, zs.at[2 * k - 2], zr.at[2 * k - 2]).wait_recv()
         if k < RING // 2:
-            z_copy(wrap(z + (k - 1), RING), down, zs.at[2 * k - 1], zr.at[2 * k - 1], True)
-
-    def z_wait(k):
-        z_copy(wrap(z - k, RING), up, zs.at[2 * k - 2], zr.at[2 * k - 2], False)
-        if k < RING // 2:
-            z_copy(wrap(z + k, RING), down, zs.at[2 * k - 1], zr.at[2 * k - 1], False)
-
-    def z_share(k):
-        z_copy(wrap(z - k, RING), other, cs.at[2 * k - 1], cr.at[2 * k - 1], True)
-        if k < RING // 2:
-            z_copy(wrap(z + k, RING), other, cs.at[2 * k], cr.at[2 * k], True)
-
-    def z_go(k):
-        z_wait(k)
-        if k < RING // 2:
+            z_copy(wrap(z + k, RING), down, zs.at[2 * k - 1], zr.at[2 * k - 1]).wait_recv()
             z_step(k + 1)
-        z_share(k)
+        for s in blocks(k):
+            for product in both:
+                product.dispatch(ring.at[s], s)
+
+    def z_collect(k):
+        for s in blocks(k):
+            for product in both:
+                product.collect(s, other)
 
     z_step(1)
-    mm.first()
-    mm.second(0)
-    gg.first()
-    uu.first()
-    gg.second(0)
-    uu.second(0)
-    z_copy(z, other, cs.at[0], cr.at[0], True)
+    for product in both:
+        product.masks.first()
+    for product in both:
+        product.dispatch(ring.at[z], z)
+    for product in both:
+        product.weights.first()
     d_copy = remote(d_in, far_d, ds.at[0], dr.at[0], other)
     d_copy.start()
-    mm.relay()
-    mm.second(1)
-    mm.second(2)
+    for product in both:
+        product.acc[...] = jnp.zeros_like(product.acc)
     z_go(1)
-    mm.relay2(0)
-    mm.far()
-    mm.second(3)
+    for product in both:
+        product.masks.relay()
     z_go(2)
-    gg.relay()
-    uu.relay()
-    gg.second(1)
-    uu.second(1)
-    gg.second(2)
-    uu.second(2)
-    for i in (1, 2, 3):
-        mm.relay2(i)
+    z_collect(0)
     z_go(3)
-    gg.relay2(0)
-    uu.relay2(0)
-    z_go(4)
-    gg.far()
-    uu.far()
-    gg.second(3)
-    uu.second(3)
-    for i in range(4):
-        mm.far2(i)
-    z_go(5)
-    gg.relay2(1)
-    uu.relay2(1)
-    z_go(6)
-    gg.relay2(2)
-    uu.relay2(2)
-    flag_copy = pltpu.make_async_copy(m, flags, ls.at[4])
-    flag_copy.start()
-    ga[...] = jnp.zeros_like(ga)
-    ua[...] = jnp.zeros_like(ua)
-    z_go(7)
-    z_go(8)
-    for n in range(RING):
-        k = (n + 1) // 2
-        block = z if n == 0 else (wrap(z - k, RING) if n % 2 else wrap(z + k, RING))
-        ref = t.at[2 * block + 1 - c]
-        remote(ref, ref, cs.at[n], cr.at[n], other).wait_recv()
-    flag_copy.wait()
-
-    def shard(dx, dy):
-        s = wrap(y + dy, SIDE) * SIDE + wrap(x + dx, SIDE)
-        w = t.shape[2]
-        for k, (buf, stage, dense, acc) in enumerate(((g, gp, gd, ga), (u, up_, ud, ua))):
-            stage[...] = buf[s].reshape(stage.shape)
-            rank = jnp.int32(0)
-            for b in range(NB * NB):
-                i, j = b // NB, b % NB
-                keep = flags[s, 0, k * NB * NB + b]
-                tile = stage[jnp.minimum(rank, CAP - 1)]
-                dense[i * BLK : (i + 1) * BLK, j * BLK : (j + 1) * BLK] = tile * keep.astype(F32).astype(BF16)
-                rank = rank + keep
-            acc[...] += jnp.dot(t[2 * s], dense[:w], preferred_element_type=F32) + jnp.dot(
-                t[2 * s + 1], dense[w:], preferred_element_type=F32
-            )
-
-    @pl.loop(0, 5)
-    def _(n):
-        sign = (1 - 2 * lax.rem(n + 1, 2)) * lax.div(n + 3, 4)
-        on_x = 1 - lax.div(n, 3)
-        shard(sign * on_x, sign * (1 - on_x))
-
-    gg.relay2(3)
-    uu.relay2(3)
-
-    @pl.loop(0, 4)
-    def _(n):
-        shard(1 - 2 * lax.rem(n, 2), 1 - 2 * lax.div(n, 2))
-
-    gg.far2(0)
-    uu.far2(0)
-
-    @pl.loop(0, 2)
-    def _(n):
-        shard(2 * n, 2 * (1 - n))
-
-    for i in (1, 2):
-        gg.far2(i)
-        uu.far2(i)
-
-    @pl.loop(0, 4)
-    def _(n):
-        sign = 1 - 2 * lax.rem(n, 2)
-        on_x = lax.div(n, 2)
-        shard(2 * on_x + sign * (1 - on_x), sign * on_x + 2 * (1 - on_x))
-
-    gg.far2(3)
-    uu.far2(3)
-    shard(2, 2)
-    gate = ga[...]
-    hidden = (gate / (1.0 + jnp.exp(-gate)) * ua[...]).astype(BF16)
-    hid[...] = hidden.reshape(hid.shape)
+    z_collect(1)
+    for product in both:
+        product.weights.relay()
+    for product in both:
+        product.masks.far()
+    flag_copies = [
+        pltpu.make_async_copy(product.m, product.flags, ls.at[i]) for i, product in enumerate(both)
+    ]
+    for cp in flag_copies:
+        cp.start()
+    for k in range(4, RING // 2 + 1):
+        z_go(k)
+        z_collect(k - 2)
+    for product in both:
+        product.weights.far()
+    z_collect(RING // 2 - 1)
+    z_collect(RING // 2)
+    for cp in flag_copies:
+        cp.wait()
+
+    for product in both:
+
+        @pl.loop(0, SIDE)
+        def _(n, product=product):
+            j = wrap(lax.div(z, SIDE) + n, SIDE)
+            product.multiply(j, other, stage, dense)
+
+        if product is up_:
+            gate.sum_relay()
+        product.sum_start()
+    up_.sum_relay()
+    for n, (a, b) in enumerate(zip(gate.total(), up_.total())):
+        hid[n] = (a / (1.0 + jnp.exp(-a)) * b).astype(BF16)
     remote(d_in, far_d, ds.at[0], dr.at[0], other).wait_recv()
     d_copy.wait_send()
-    mm.drain()
-    gg.drain()
-    uu.drain()
+    for product in both:
+        product.drain(other)
     for cp in sends:
         cp.wait_send()
 
@@ -361,35 +416,47 @@
 def make_hidden(m, g, u, t, d):
     dma = pltpu.SemaphoreType.DMA
     rows, width = t.shape
-    chips = SIDE * SIDE
-    hid, far_d, _ = pl.pallas_call(
+    product = [
+        pltpu.VMEM((SIDE, PACK, BLK), BF16),
+        pltpu.VMEM((SIDE, 2, SIDE, rows, width), BF16),
+        pltpu.VMEM((SIDE, rows, SHARD), F32),
+        pltpu.VMEM((2, rows // 2, SHARD), F32),
+        pltpu.VMEM((4, rows // 2, SHARD), F32),
+        pltpu.SMEM((SIDE,) + m.shape, jnp.int32),
+        dma((4,)),
+        dma((4,)),
+        dma((4,)),
+        dma((4,)),
+        dma((SIDE, SIDE)),
+        dma((SIDE, SIDE)),
+        dma((SIDE,)),
+        dma((SIDE,)),
+        dma((SIDE,)),
+        dma((6,)),
+        dma((6,)),
+    ]
+    hid, far_d, _, _ = pl.pallas_call(
         hidden_kernel,
         out_shape=[
             jax.ShapeDtypeStruct((2, rows // 2, SHARD), BF16),
             jax.ShapeDtypeStruct(d.shape, BF16),
-            jax.ShapeDtypeStruct((chips,) + m.shape, m.dtype),
+            jax.ShapeDtypeStruct((SIDE,) + m.shape, m.dtype),
+            jax.ShapeDtypeStruct((SIDE,) + m.shape, m.dtype),
         ],
         in_specs=[pl.BlockSpec(memory_space=HBM)] * 5,
         out_specs=[
             pl.BlockSpec(memory_space=VMEM),
             pl.BlockSpec(memory_space=HBM),
             pl.BlockSpec(memory_space=HBM),
+            pl.BlockSpec(memory_space=HBM),
         ],
         scratch_shapes=[
-            pltpu.VMEM((chips, PACK, BLK), BF16),
-            pltpu.VMEM((chips, PACK, BLK), BF16),
-            pltpu.VMEM((2 * RING, rows, width), BF16),
-            pltpu.VMEM((CAP, BLK, BLK), BF16),
+            pltpu.VMEM((RING, rows, width), BF16),
             pltpu.VMEM((CAP, BLK, BLK), BF16),
             pltpu.VMEM((SHARD, SHARD), BF16),
-            pltpu.VMEM((SHARD, SHARD), BF16),
-            pltpu.VMEM((rows, SHARD), F32),
-            pltpu.VMEM((rows, SHARD), F32),
-            pltpu.SMEM((chips,) + m.shape, jnp.int32),
         ]
-        + [dma((20,))] * 6
+        + product * 2
         + [dma((15,))] * 2
-        + [dma((16,))] * 2
         + [dma((1,))] * 2
         + [dma((5,))],
         compiler_params=pltpu.CompilerParams(collective_id=0, has_side_effects=True, vmem_limit_bytes=48 << 20),
@@ -398,18 +465,22 @@
     return hid, far_d
 
 
-PARTS = 2
+PARTS = 1
+CHAINS = 4
+LAG = 2
+EARLY = 0
 
 
 def tail_kernel(
-    hid, d_own, d_far, o_ref, ha, hb, p, up_buf, down_buf,
-    as0, ar0, as1, ar1, bs0, br0, bs1, br1, ps, pr, us, ur, ds, dr, ls,
+    hid, d_own, d_far, o_ref, ha, hb, p, up_in, up_out, down_in, down_out, up_in16, up_out16, down_in16, down_out16,
+    gs, gr, ps, pr, us, ur, ds, dr, ls,
 ):
     x, y, z, c = place()
     up, down = device(x, y, wrap(z + 1, RING), c), device(x, y, wrap(z - 1, RING), c)
     other = device(x, y, z, 1 - c)
     me = y * SIDE + x
     piece = ha.shape[2]
+    bit = piece // CHAINS
     own = [
         pltpu.make_async_copy(hid.at[c, pl.ds(q * piece, piece)], ha.at[q, me], ls.at[q]) for q in range(PARTS)
     ]
@@ -433,8 +504,8 @@
         cp.start()
     for cp in own:
         cp.wait()
-    a = [Gather(ha.at[q], piece, True, s, r) for q, (s, r) in enumerate(((as0, ar0), (as1, ar1)))]
-    b = [Gather(hb.at[q], piece, False, s, r) for q, (s, r) in enumerate(((bs0, br0), (bs1, br1)))]
+    a = [Gather(ha.at[q], piece, True, gs.at[q], gr.at[q]) for q in range(PARTS)]
+    b = [Gather(hb.at[q], piece, False, gs.at[PARTS + q], gr.at[PARTS + q]) for q in range(PARTS)]
     sends = []
     far_up, far_down = RING // 2, RING // 2 - 1
 
@@ -462,6 +533,26 @@
         for i in (1, 2, 3):
             for s in (a[q], b[q]):
                 s.relay2(i)
+
+    def ways(q, r):
+        n = q * CHAINS + r
+        return (
+            (up_in, up_out, up_in16, up_out16, up, us.at[n], ur.at[n], far_up, 1),
+            (down_in, down_out, down_in16, down_out16, down, ds.at[n], dr.at[n], far_down, -1),
+        )
+
+    def hop(k, n, way):
+        wide_in, wide_out, thin_in, thin_out, dev, ss, rs, _, _ = way
+        if k < EARLY:
+            return thin_out.at[k, n], remote(thin_out.at[k, n], thin_in.at[k, n], ss.at[k], rs.at[k], dev)
+        return wide_out.at[k - EARLY, n], remote(wide_out.at[k - EARLY, n], wide_in.at[k - EARLY, n], ss.at[k], rs.at[k], dev)
+
+    def arrived(k, n, way):
+        hop(k, n, way)[1].wait_recv()
+        return way[2][k, n].astype(F32) if k < EARLY else way[0][k - EARLY, n]
+
+    def mine(q, r, block):
+        return p[q, block, r * bit : (r + 1) * bit]
 
     def end(q):
         for i in range(4):
@@ -476,57 +567,49 @@
             right, d_far[...], preferred_element_type=F32
         )
         p[q] = sums.reshape(p.shape[1:])
-
-    def ring(buf, step, q, dev, ss, rs, src):
-        n = step * PARTS + q
-        return remote(src, buf.at[step, q], ss.at[n], rs.at[n], dev)
-
-    def push(q):
-        for buf, dev, ss, rs, block in (
-            (up_buf, up, us, ur, wrap(z + far_up, RING)),
-            (down_buf, down, ds, dr, wrap(z - far_down, RING)),
-        ):
-            cp = ring(buf, 0, q, dev, ss, rs, p.at[q, block])
-            cp.start()
-            sends.append(cp)
-
-    def step(k, q):
-        for buf, dev, ss, rs, far, block in (
-            (up_buf, up, us, ur, far_up, wrap(z + far_up - k, RING)),
-            (down_buf, down, ds, dr, far_down, wrap(z - far_down + k, RING)),
-        ):
-            if k > far:
-                continue
-            here = buf.at[k - 1, q]
-            ring(buf, k - 1, q, dev, ss, rs, here).wait_recv()
-            if k < far:
-                buf[k - 1, q] += p[q, block]
-                cp = ring(buf, k, q, dev, ss, rs, here)
+        for r in range(CHAINS):
+            n = q * CHAINS + r
+            for way in ways(q, r):
+                ref, cp = hop(0, n, way)
+                ref[...] = mine(q, r, wrap(z + way[-1] * way[-2], RING)).astype(ref.dtype)
                 cp.start()
                 sends.append(cp)
-        if k == far_up:
-            total = p[q, z] + up_buf[far_up - 1, q] + down_buf[far_down - 1, q]
-            o_ref[q * piece : (q + 1) * piece, :] = total.astype(BF16)
-
-    begin(0)
-    near(0)
-    begin(1)
-    middle(0)
-    near(1)
-    late(0)
-    middle(1)
-    end(0)
-    multiply(0)
-    push(0)
-    late(1)
-    step(1, 0)
-    end(1)
-    multiply(1)
-    push(1)
-    for k in range(2, far_up + 1):
-        step(k, 0)
-        step(k - 1, 1)
-    step(far_up, 1)
+
+    def step(k, q):
+        for r in range(CHAINS):
+            n = q * CHAINS + r
+            for way in ways(q, r):
+                far, sign = way[-2], way[-1]
+                if k < far:
+                    total = arrived(k - 1, n, way) + mine(q, r, wrap(z + sign * (far - k), RING))
+                    ref, cp = hop(k, n, way)
+                    ref[...] = total.astype(ref.dtype)
+                    cp.start()
+                    sends.append(cp)
+            if k == far_up:
+                total = mine(q, r, z)
+                for way in ways(q, r):
+                    total = total + arrived(way[-2] - 1, n, way)
+                row = q * piece + r * bit
+                o_ref[row : row + bit, :] = total.astype(BF16)
+
+    stages = (begin, near, middle, late, end, multiply)
+    at = [0] * PARTS
+    for tick in range(LAG * (PARTS - 1) + len(stages)):
+        for q in range(PARTS):
+            if at[q] and at[q] <= far_up:
+                step(at[q], q)
+                at[q] += 1
+        for q in range(PARTS):
+            n = tick - LAG * q
+            if 0 <= n < len(stages):
+                stages[n](q)
+                at[q] = int(n == len(stages) - 1)
+    while min(at) <= far_up:
+        for q in range(PARTS):
+            if at[q] <= far_up:
+                step(at[q], q)
+                at[q] += 1
     for cp in swaps:
         cp.wait_send()
     for s in a + b:
@@ -542,6 +625,8 @@
     chips = SIDE * SIDE
     n_up, n_down = RING // 2, RING // 2 - 1
     piece = rows // PARTS
+    chains = PARTS * CHAINS
+    bit = piece // CHAINS
     return pl.pallas_call(
         tail_kernel,
         out_shape=jax.ShapeDtypeStruct((rows, cols), BF16),
@@ -551,13 +636,13 @@
             pltpu.VMEM((PARTS, chips, piece, width), BF16),
             pltpu.VMEM((PARTS, chips, piece, width), BF16),
             pltpu.VMEM((PARTS, chips, piece, cols), F32),
-            pltpu.VMEM((n_up, PARTS, piece, cols), F32),
-            pltpu.VMEM((n_down, PARTS, piece, cols), F32),
         ]
-        + [dma((20,))] * 8
+        + [pltpu.VMEM((max(n - EARLY, 1), chains, bit, cols), F32) for n in (n_up, n_up, n_down, n_down)]
+        + [pltpu.VMEM((max(EARLY, 1), chains, bit, cols), BF16) for _ in range(4)]
+        + [dma((2 * PARTS, 20))] * 2
         + [dma((PARTS,))] * 2
-        + [dma((n_up * PARTS,))] * 2
-        + [dma((n_down * PARTS,))] * 2
+        + [dma((chains, n_up))] * 2
+        + [dma((chains, n_down))] * 2
         + [dma((PARTS,))],
         compiler_params=pltpu.CompilerParams(collective_id=1, has_side_effects=True, vmem_limit_bytes=48 << 20),
         name="tail",

time: 128 us -> 129 us (level)
    pallas_call x1, Pallas kernels: 64.5 us -> 70.4 us  [make_hidden(): pl.pallas_call(hidden_kernel, out_shape=[jax.ShapeDtypeStruct((2, rows //...]
    pallas_call x1, Pallas kernels: 56.6 us -> 51.4 us  [tail(): pl.pallas_call(tail_kernel, out_shape=jax.ShapeDtypeStruct((rows, cols),...]
where the time goes in v3:
time: 129 us
  Pallas kernels  125 us (97%)
  local copies, waits for them, and re-layouts  4.23 us (3%)
    pallas_call x1, Pallas kernels, make_hidden(): pl.pallas_call(hidden_kernel, out_shape=[jax.ShapeDtypeStruct((2, rows //...  70.4 us
    pallas_call x1, Pallas kernels, tail(): pl.pallas_call(tail_kernel, out_shape=jax.ShapeDtypeStruct((rows, cols),...  51.4 us
    unnamed x13, local copies, waits for them, and re-layouts  4.23 us
    pallas_call x1, Pallas kernels, pack(): pl.pallas_call(pack_kernel, in_specs=[pl.BlockSpec(memory_space=pltpu.Mem...  2.86 us

profile of v3, /device:TPU:6, one launch (start us, length us, event | category | flops | bytes accessed | tf_op | source)
XLA Modules:
  0.0 128.9 jit_solution(12458636078020716499)
XLA Ops:
  0.0 0.0 copy-start.4
  0.0 2.9 %pack.1 = (s32[1,128]{1,0:T(1,128)}, bf16[1024,128]{1,0:T(8,128)(2,1)}, bf16[1024,128]{1,0:T(8,128)(2,1)}, bf16[512,512]{1,0:T(8,128)(2,1)}) custom-call(s32[4,4]{1,0:T(4,128)} %gk_ref.1, s32[4,4]{1,0:T(4,128)} %uk_ref.1, s32[4,4]{1,0:T(4,128)} %dk_ref.1, bf16[512,512]{1,0:T(8,128)(2,1)} %gw_ref.1, bf16[512,512]{1,0:T(8,128)(2,1)} %uw_ref.1, ...), custom_call_target="tpu_custom_call" | custom-call | tf_op jit(solution)/shard_map/pack/pallas_call | solution.py:163
  2.9 0.0 copy-start.5
  2.9 0.0 copy-done.4
  2.9 0.7 copy-done.5
  3.5 0.0 copy-start
  3.5 1.0 copy-done
  4.6 0.0 copy-start.2
  4.6 0.9 copy-done.2
  5.5 0.0 copy-start.3
  5.5 0.9 copy-done.3
  6.5 0.0 copy-start.1
  6.5 70.4 %make_hidden.1 = (bf16[2,64,512]{2,1,0:T(8,128)(2,1)S(1)}, bf16[512,512]{1,0:T(8,128)(2,1)S(1)}, s32[4,1,128]{2,1,0:T(1,128)}, s32[4,1,128]{2,1,0:T(1,128)}) custom-call(s32[1,128]{1,0:T(1,128)S(1)} %copy-done.5, bf16[1024,128]{1,0:T(8,128)(2,1)S(1)} %copy-done.2, bf16[1024,128]{1,0:T(8,128)(2,1)S(1)} %copy-done.3, bf16[128,256]{1,0:T(8,128)(2,1)S(1)} %copy-done.4, ...), custom_call_target="tpu_custom_call" | custom-call | tf_op jit(solution)/shard_map/make_hidden/pallas_call | solution.py:438
  76.9 0.0 copy-done.1
  76.9 51.4 %tail.1 = bf16[64,512]{1,0:T(8,128)(2,1)S(1)} custom-call(bf16[2,64,512]{2,1,0:T(8,128)(2,1)S(1)} %get-tuple-element.15.hid, bf16[512,512]{1,0:T(8,128)(2,1)S(1)} %copy-done.1, bf16[512,512]{1,0:T(8,128)(2,1)S(1)} %get-tuple-element.16.d_far), custom_call_target="tpu_custom_call" | custom-call | tf_op jit(solution)/shard_map/tail/pallas_call | solution.py:630
  128.3 0.6 copy.9
Async XLA Ops:
  0.0 2.9 %copy-start.4 = (bf16[128,256]{1,0:T(8,128)(2,1)S(1)}, bf16[128,256]{1,0:T(8,128)(2,1)}, u32[]{:S(2)}) copy-start(bf16[128,256]{1,0:T(8,128)(2,1)} %t_in.1) | copy-start | bytes 196612
  2.9 0.7 copy-start.5
  3.5 1.0 copy-start
  4.6 0.9 copy-start.2
  5.5 0.9 copy-start.3
  6.5 70.4 %copy-start.1 = (bf16[512,512]{1,0:T(8,128)(2,1)S(1)}, bf16[512,512]{1,0:T(8,128)(2,1)}, u32[]{:S(2)}) copy-start(bf16[512,512]{1,0:T(8,128)(2,1)} %get-tuple-element.14.d_in.d_own) | copy-start | bytes 1572868

commit v4 on v3

--- a/solution.py
+++ b/solution.py
@@ -10,6 +10,7 @@
 MESH = pl.DeviceIdType.MESH
 HBM = pltpu.MemorySpace.HBM
 VMEM = pltpu.MemorySpace.VMEM
+INPUTS = HBM
 BF16 = jnp.bfloat16
 F32 = jnp.float32
 
@@ -20,6 +21,7 @@
 CAP = 8
 SHARD = NB * BLK
 PACK = CAP * BLK
+PIECES = 4
 
 
 def place():
@@ -135,11 +137,18 @@
             cp.wait_send()
 
 
-def pack_kernel(gk_ref, uk_ref, dk_ref, gw_ref, uw_ref, dw_ref, m_ref, g_ref, u_ref, d_ref):
+def pack_kernel(gk_ref, uk_ref, dk_ref, gw_in, uw_in, dw_in, m_ref, g_ref, u_ref, d_ref, gw_ref, uw_ref, dw_ref, sem):
+    loads = [
+        pltpu.make_async_copy(src, dst, sem.at[i])
+        for i, (src, dst) in enumerate(((gw_in, gw_ref), (uw_in, uw_ref), (dw_in, dw_ref)))
+    ]
+    for cp in loads:
+        cp.start()
     lane = lax.broadcasted_iota(jnp.int32, m_ref.shape, 1)
     flags = jnp.zeros(m_ref.shape, jnp.int32)
     for m, (keep_ref, w_ref, o_ref) in enumerate(((gk_ref, gw_ref, g_ref), (uk_ref, uw_ref, u_ref))):
         o_ref[...] = jnp.zeros_like(o_ref)
+        loads[m].wait()
         rank = jnp.int32(0)
         for b in range(NB * NB):
             i, j = b // NB, b % NB
@@ -153,6 +162,7 @@
             flags = jnp.where(lane == m * NB * NB + b, keep, flags)
             rank = rank + keep
     m_ref[...] = flags
+    loads[2].wait()
     for i in range(NB):
         for j in range(NB):
             r, s = slice(i * BLK, (i + 1) * BLK), slice(j * BLK, (j + 1) * BLK)
@@ -162,7 +172,8 @@
 def pack(gw, uw, dw, gk, uk, dk):
     return pl.pallas_call(
         pack_kernel,
-        in_specs=[pl.BlockSpec(memory_space=pltpu.MemorySpace.SMEM)] * 3 + [pl.BlockSpec(memory_space=VMEM)] * 3,
+        in_specs=[pl.BlockSpec(memory_space=pltpu.MemorySpace.SMEM)] * 3 + [pl.BlockSpec(memory_space=HBM)] * 3,
+        scratch_shapes=[pltpu.VMEM(w.shape, w.dtype) for w in (gw, uw, dw)] + [pltpu.SemaphoreType.DMA((3,))],
         out_specs=[pl.BlockSpec(memory_space=VMEM)] * 4,
         out_shape=[
             jax.ShapeDtypeStruct((1, BLK), jnp.int32),
@@ -293,7 +304,7 @@
         self.masks.drain()
 
 
-def hidden_kernel(m_in, g_in, u_in, t_in, d_in, hid, far_d, mg, mu, ring, stage, dense, *refs):
+def hidden_phase(m_in, g_in, u_in, t_in, d_in, mg, mu, hid, d_own, d_far, ring, stage, dense, *refs):
     x, y, z, c = place()
     zs, zr, ds, dr, ls = refs[-5:]
     per = len(refs[:-5]) // 2
@@ -311,6 +322,7 @@
                 (u_in, up_.w.at[x]),
                 (m_in, gate.m.at[y]),
                 (m_in, up_.m.at[x]),
+                (d_in, d_own),
             )
         )
     ]
@@ -326,15 +338,16 @@
     sends = []
     both = (gate, up_)
 
-    def z_copy(block, dev, send, recv):
-        return remote(ring.at[block], ring.at[block], send, recv, dev)
-
-    def z_step(k):
-        cp = z_copy(wrap(z - (k - 1), RING), up, zs.at[2 * k - 2], zr.at[2 * k - 2])
-        cp.start()
-        sends.append(cp)
-        if k < RING // 2:
-            cp = z_copy(wrap(z + (k - 1), RING), down, zs.at[2 * k - 1], zr.at[2 * k - 1])
+    size = t_in.shape[0] // PIECES
+
+    def z_copy(k, p, sign, block):
+        ref = ring.at[block, pl.ds(p * size, size)]
+        n = 2 * k - 2 if sign > 0 else 2 * k - 1
+        return remote(ref, ref, zs.at[n, p], zr.at[n, p], up if sign > 0 else down)
+
+    def z_step(k, p):
+        for sign in (1, -1) if k < RING // 2 else (1,):
+            cp = z_copy(k, p, sign, wrap(z - sign * (k - 1), RING))
             cp.start()
             sends.append(cp)
 
@@ -342,10 +355,11 @@
         return (wrap(z - k, RING), wrap(z + k, RING))[: 1 if k in (0, RING // 2) else 2]
 
     def z_go(k):
-        z_copy(wrap(z - k, RING), up, zs.at[2 * k - 2], zr.at[2 * k - 2]).wait_recv()
-        if k < RING // 2:
-            z_copy(wrap(z + k, RING), down, zs.at[2 * k - 1], zr.at[2 * k - 1]).wait_recv()
-            z_step(k + 1)
+        for p in range(PIECES):
+            for sign in (1, -1) if k < RING // 2 else (1,):
+                z_copy(k, p, sign, wrap(z - sign * k, RING)).wait_recv()
+            if k < RING // 2:
+                z_step(k + 1, p)
         for s in blocks(k):
             for product in both:
                 product.dispatch(ring.at[s], s)
@@ -355,14 +369,15 @@
             for product in both:
                 product.collect(s, other)
 
-    z_step(1)
+    for p in range(PIECES):
+        z_step(1, p)
     for product in both:
         product.masks.first()
     for product in both:
         product.dispatch(ring.at[z], z)
     for product in both:
         product.weights.first()
-    d_copy = remote(d_in, far_d, ds.at[0], dr.at[0], other)
+    d_copy = remote(d_in, d_far, ds.at[0], dr.at[0], other)
     d_copy.start()
     for product in both:
         product.acc[...] = jnp.zeros_like(product.acc)
@@ -405,64 +420,12 @@
     up_.sum_relay()
     for n, (a, b) in enumerate(zip(gate.total(), up_.total())):
         hid[n] = (a / (1.0 + jnp.exp(-a)) * b).astype(BF16)
-    remote(d_in, far_d, ds.at[0], dr.at[0], other).wait_recv()
+    d_copy.wait_recv()
     d_copy.wait_send()
     for product in both:
         product.drain(other)
     for cp in sends:
         cp.wait_send()
-
-
-def make_hidden(m, g, u, t, d):
-    dma = pltpu.SemaphoreType.DMA
-    rows, width = t.shape
-    product = [
-        pltpu.VMEM((SIDE, PACK, BLK), BF16),
-        pltpu.VMEM((SIDE, 2, SIDE, rows, width), BF16),
-        pltpu.VMEM((SIDE, rows, SHARD), F32),
-        pltpu.VMEM((2, rows // 2, SHARD), F32),
-        pltpu.VMEM((4, rows // 2, SHARD), F32),
-        pltpu.SMEM((SIDE,) + m.shape, jnp.int32),
-        dma((4,)),
-        dma((4,)),
-        dma((4,)),
-        dma((4,)),
-        dma((SIDE, SIDE)),
-        dma((SIDE, SIDE)),
-        dma((SIDE,)),
-        dma((SIDE,)),
-        dma((SIDE,)),
-        dma((6,)),
-        dma((6,)),
-    ]
-    hid, far_d, _, _ = pl.pallas_call(
-        hidden_kernel,
-        out_shape=[
-            jax.ShapeDtypeStruct((2, rows // 2, SHARD), BF16),
-            jax.ShapeDtypeStruct(d.shape, BF16),
-            jax.ShapeDtypeStruct((SIDE,) + m.shape, m.dtype),
-            jax.ShapeDtypeStruct((SIDE,) + m.shape, m.dtype),
-        ],
-        in_specs=[pl.BlockSpec(memory_space=HBM)] * 5,
-        out_specs=[
-            pl.BlockSpec(memory_space=VMEM),
-            pl.BlockSpec(memory_space=HBM),
-            pl.BlockSpec(memory_space=HBM),
-            pl.BlockSpec(memory_space=HBM),
-        ],
-        scratch_shapes=[
-            pltpu.VMEM((RING, rows, width), BF16),
-            pltpu.VMEM((CAP, BLK, BLK), BF16),
-            pltpu.VMEM((SHARD, SHARD), BF16),
-        ]
-        + product * 2
-        + [dma((15,))] * 2
-        + [dma((1,))] * 2
-        + [dma((5,))],
-        compiler_params=pltpu.CompilerParams(collective_id=0, has_side_effects=True, vmem_limit_bytes=48 << 20),
-        name="make_hidden",
-    )(m, g, u, t, d)
-    return hid, far_d
 
 
 PARTS = 1
@@ -471,7 +434,7 @@
 EARLY = 0
 
 
-def tail_kernel(
+def tail_phase(
     hid, d_own, d_far, o_ref, ha, hb, p, up_in, up_out, down_in, down_out, up_in16, up_out16, down_in16, down_out16,
     gs, gr, ps, pr, us, ur, ds, dr, ls,
 ):
@@ -486,17 +449,6 @@
     ]
     for cp in own:
         cp.start()
-    greet(
-        (
-            device(wrap(x + 1, SIDE), y, z, c),
-            device(wrap(x - 1, SIDE), y, z, c),
-            device(x, wrap(y + 1, SIDE), z, c),
-            device(x, wrap(y - 1, SIDE), z, c),
-            up,
-            down,
-            other,
-        )
-    )
     swaps = [
         remote(hid.at[1 - c, pl.ds(q * piece, piece)], hb.at[q, me], ps.at[q], pr.at[q], other) for q in range(PARTS)
     ]
@@ -618,23 +570,62 @@
         cp.wait_send()
 
 
-def tail(hid, d_own, d_far):
+def layer_kernel(*refs):
+    ins, o_ref, masks = refs[:5], refs[5], refs[6:8]
+    kept, first, last = refs[8:11], refs[11 : 11 + N_FIRST], refs[11 + N_FIRST :]
+    hidden_phase(*ins, *masks, *kept, *first)
+    tail_phase(*kept, o_ref, *last)
+
+
+N_FIRST = 3 + 2 * 17 + 5
+
+
+def layer(m, g, u, t, d):
     dma = pltpu.SemaphoreType.DMA
-    _, rows, width = hid.shape
-    cols = d_own.shape[1]
+    rows, width = t.shape
+    cols = d.shape[1]
     chips = SIDE * SIDE
     n_up, n_down = RING // 2, RING // 2 - 1
-    piece = rows // PARTS
+    half = rows // 2
+    piece = half // PARTS
     chains = PARTS * CHAINS
     bit = piece // CHAINS
-    return pl.pallas_call(
-        tail_kernel,
-        out_shape=jax.ShapeDtypeStruct((rows, cols), BF16),
-        in_specs=[pl.BlockSpec(memory_space=HBM)] + [pl.BlockSpec(memory_space=VMEM)] * 2,
-        out_specs=pl.BlockSpec(memory_space=VMEM),
-        scratch_shapes=[
-            pltpu.VMEM((PARTS, chips, piece, width), BF16),
-            pltpu.VMEM((PARTS, chips, piece, width), BF16),
+    product = [
+        pltpu.VMEM((SIDE, PACK, BLK), BF16),
+        pltpu.VMEM((SIDE, 2, SIDE, rows, width), BF16),
+        pltpu.VMEM((SIDE, rows, SHARD), F32),
+        pltpu.VMEM((2, half, SHARD), F32),
+        pltpu.VMEM((4, half, SHARD), F32),
+        pltpu.SMEM((SIDE,) + m.shape, jnp.int32),
+        dma((4,)),
+        dma((4,)),
+        dma((4,)),
+        dma((4,)),
+        dma((SIDE, SIDE)),
+        dma((SIDE, SIDE)),
+        dma((SIDE,)),
+        dma((SIDE,)),
+        dma((SIDE,)),
+        dma((6,)),
+        dma((6,)),
+    ]
+    kept = [pltpu.VMEM((2, half, SHARD), BF16), pltpu.VMEM(d.shape, BF16), pltpu.VMEM(d.shape, BF16)]
+    first = (
+        [
+            pltpu.VMEM((RING, rows, width), BF16),
+            pltpu.VMEM((CAP, BLK, BLK), BF16),
+            pltpu.VMEM((SHARD, SHARD), BF16),
+        ]
+        + product * 2
+        + [dma((RING - 1, PIECES))] * 2
+        + [dma((1,))] * 2
+        + [dma((6,))]
+    )
+    assert len(first) == N_FIRST
+    last = (
+        [
+            pltpu.VMEM((PARTS, chips, piece, SHARD), BF16),
+            pltpu.VMEM((PARTS, chips, piece, SHARD), BF16),
             pltpu.VMEM((PARTS, chips, piece, cols), F32),
         ]
         + [pltpu.VMEM((max(n - EARLY, 1), chains, bit, cols), F32) for n in (n_up, n_up, n_down, n_down)]
@@ -643,16 +634,31 @@
         + [dma((PARTS,))] * 2
         + [dma((chains, n_up))] * 2
         + [dma((chains, n_down))] * 2
-        + [dma((PARTS,))],
-        compiler_params=pltpu.CompilerParams(collective_id=1, has_side_effects=True, vmem_limit_bytes=48 << 20),
-        name="tail",
-    )(hid, d_own, d_far)
+        + [dma((PARTS,))]
+    )
+    out, _, _ = pl.pallas_call(
+        layer_kernel,
+        out_shape=[
+            jax.ShapeDtypeStruct((half, cols), BF16),
+            jax.ShapeDtypeStruct((SIDE,) + m.shape, m.dtype),
+            jax.ShapeDtypeStruct((SIDE,) + m.shape, m.dtype),
+        ],
+        in_specs=[pl.BlockSpec(memory_space=INPUTS)] * 5,
+        out_specs=[
+            pl.BlockSpec(memory_space=VMEM),
+            pl.BlockSpec(memory_space=HBM),
+            pl.BlockSpec(memory_space=HBM),
+        ],
+        scratch_shapes=kept + first + last,
+        compiler_params=pltpu.CompilerParams(collective_id=0, has_side_effects=True, vmem_limit_bytes=48 << 20),
+        name="layer",
+    )(m, g, u, t, d)
+    return out
 
 
 def local(tokens, gate_weight, up_weight, down_weight, gate_keep, up_keep, down_keep):
     m, g, u, d = pack(gate_weight, up_weight, down_weight, gate_keep, up_keep, down_keep)
-    hid, far_d = make_hidden(m, g, u, tokens, d)
-    return tail(hid, d, far_d)
+    return layer(m, g, u, tokens, d)
 
 
 def solution(mesh):

time: 129 us -> 125 us (0.969)
  Pallas kernels: 125 us -> 121 us
    pallas_call x2 -> x1, Pallas kernels: 122 us -> 117 us  [layer(): pl.pallas_call(layer_kernel, out_shape=[jax.ShapeDtypeStruct((half, cols)...]
    unnamed x13 -> x11, local copies, waits for them, and re-layouts: 4.23 us -> 4.22 us
where the time goes in v4:
time: 125 us
  Pallas kernels  121 us (97%)
  local copies, waits for them, and re-layouts  4.22 us (3%)
    pallas_call x1, Pallas kernels, layer(): pl.pallas_call(layer_kernel, out_shape=[jax.ShapeDtypeStruct((half, cols)...  117 us
    unnamed x11, local copies, waits for them, and re-layouts  4.22 us
    pallas_call x1, Pallas kernels, pack(): pl.pallas_call(pack_kernel, in_specs=[pl.BlockSpec(memory_space=pltpu.Mem...  3.37 us

profile of v4, /device:TPU:6, one launch (start us, length us, event | category | flops | bytes accessed | tf_op | source)
XLA Modules:
  0.0 124.9 jit_solution(12234973785886815677)
XLA Ops:
  0.0 0.0 copy-start.3
  0.0 3.4 %pack.1 = (s32[1,128]{1,0:T(1,128)}, bf16[1024,128]{1,0:T(8,128)(2,1)}, bf16[1024,128]{1,0:T(8,128)(2,1)}, bf16[512,512]{1,0:T(8,128)(2,1)}) custom-call(s32[4,4]{1,0:T(4,128)} %gk_ref.1, s32[4,4]{1,0:T(4,128)} %uk_ref.1, s32[4,4]{1,0:T(4,128)} %dk_ref.1, bf16[512,512]{1,0:T(8,128)(2,1)} %gw_in.1, bf16[512,512]{1,0:T(8,128)(2,1)} %uw_in.1, ...), custom_call_target="tpu_custom_call" | custom-call | tf_op jit(solution)/shard_map/pack/pallas_call | solution.py:173
  3.4 0.0 copy-start.4
  3.4 0.0 copy-done.3
  3.4 0.6 copy-done.4
  4.0 0.0 copy-start
  4.0 1.0 copy-done
  5.1 0.0 copy-start.1
  5.1 0.9 copy-done.1
  6.0 0.0 copy-start.2
  6.0 0.9 copy-done.2
  7.0 117.3 %layer.1 = (bf16[64,512]{1,0:T(8,128)(2,1)S(1)}, s32[4,1,128]{2,1,0:T(1,128)}, s32[4,1,128]{2,1,0:T(1,128)}) custom-call(s32[1,128]{1,0:T(1,128)S(1)} %copy-done.4, bf16[1024,128]{1,0:T(8,128)(2,1)S(1)} %copy-done.1, bf16[1024,128]{1,0:T(8,128)(2,1)S(1)} %copy-done.2, bf16[128,256]{1,0:T(8,128)(2,1)S(1)} %copy-done.3, bf16[512,512]{1,0:T(8,128)(2,1)S(1)} %copy-done), custom_call_target="tpu_custom_call" | custom-call | tf_op jit(solution)/shard_map/layer/pallas_call | solution.py:639
  124.3 0.6 copy.9
Async XLA Ops:
  0.0 3.4 %copy-start.3 = (bf16[128,256]{1,0:T(8,128)(2,1)S(1)}, bf16[128,256]{1,0:T(8,128)(2,1)}, u32[]{:S(2)}) copy-start(bf16[128,256]{1,0:T(8,128)(2,1)} %refs_3_.1) | copy-start | bytes 196612
  3.4 0.7 copy-start.4
  4.0 1.0 copy-start
  5.1 0.9 copy-start.1
  6.0 0.9 copy-start.2

commit v5 on v4

--- a/solution.py
+++ b/solution.py
@@ -21,7 +21,6 @@
 CAP = 8
 SHARD = NB * BLK
 PACK = CAP * BLK
-PIECES = 4
 
 
 def place():
@@ -311,7 +310,6 @@
     g_refs, u_refs = refs[:per], refs[per : 2 * per]
     gate = Product(True, (g_refs[0], mg) + g_refs[1:])
     up_ = Product(False, (u_refs[0], mu) + u_refs[1:])
-    up, down = device(x, y, wrap(z + 1, RING), c), device(x, y, wrap(z - 1, RING), c)
     other = device(x, y, z, 1 - c)
     own = [
         pltpu.make_async_copy(src, dst, ls.at[i])
@@ -331,65 +329,68 @@
     greet(
         [device(wrap(x + k, SIDE), y, z, c) for k in (1, 2, 3)]
         + [device(x, wrap(y + k, SIDE), z, c) for k in (1, 2, 3)]
-        + [up, down, other]
+        + [device(x, y, wrap(z + k, RING), c) for k in (1, 2, -1, -2)]
+        + [other]
     )
     for cp in own:
         cp.wait()
     sends = []
     both = (gate, up_)
 
-    size = t_in.shape[0] // PIECES
-
-    def z_copy(k, p, sign, block):
-        ref = ring.at[block, pl.ds(p * size, size)]
-        n = 2 * k - 2 if sign > 0 else 2 * k - 1
-        return remote(ref, ref, zs.at[n, p], zr.at[n, p], up if sign > 0 else down)
-
-    def z_step(k, p):
-        for sign in (1, -1) if k < RING // 2 else (1,):
-            cp = z_copy(k, p, sign, wrap(z - sign * (k - 1), RING))
-            cp.start()
-            sends.append(cp)
-
-    def blocks(k):
-        return (wrap(z - k, RING), wrap(z + k, RING))[: 1 if k in (0, RING // 2) else 2]
-
-    def z_go(k):
-        for p in range(PIECES):
-            for sign in (1, -1) if k < RING // 2 else (1,):
-                z_copy(k, p, sign, wrap(z - sign * k, RING)).wait_recv()
-            if k < RING // 2:
-                z_step(k + 1, p)
-        for s in blocks(k):
+    def z_copy(d, have):
+        ref = ring.at[wrap(z - have, RING)]
+        n = 2 * d - 2 if d > 0 else -2 * d - 1
+        return remote(ref, ref, zs.at[n], zr.at[n], device(x, y, wrap(z + d - have, RING), c))
+
+    def z_send(d, have):
+        cp = z_copy(d, have)
+        cp.start()
+        sends.append(cp)
+
+    def z_wait(d):
+        z_copy(d, d - (1 if d > 0 else -1)).wait_recv()
+
+    def dispatch(*ds):
+        for d in ds:
             for product in both:
-                product.dispatch(ring.at[s], s)
-
-    def z_collect(k):
-        for s in blocks(k):
+                product.dispatch(ring.at[wrap(z - d, RING)], wrap(z - d, RING))
+
+    def collect(*ds):
+        for d in ds:
             for product in both:
-                product.collect(s, other)
-
-    for p in range(PIECES):
-        z_step(1, p)
+                product.collect(wrap(z - d, RING), other)
+
+    def z_go(far):
+        for sign in (1, -1):
+            d = sign * far
+            z_wait(d)
+            if far + 2 <= (RING // 2 if sign > 0 else RING // 2 - 1):
+                z_send(d + 2 * sign, d)
+            z_send(d + sign, d)
+        dispatch(far, -far)
+        for sign in (1, -1):
+            z_wait(sign * (far - 1))
+        dispatch(far - 1, 1 - far)
+
+    for d in (2, -2, 1, -1):
+        z_send(d, 0)
     for product in both:
         product.masks.first()
-    for product in both:
-        product.dispatch(ring.at[z], z)
+    dispatch(0)
     for product in both:
         product.weights.first()
     d_copy = remote(d_in, d_far, ds.at[0], dr.at[0], other)
     d_copy.start()
     for product in both:
         product.acc[...] = jnp.zeros_like(product.acc)
-    z_go(1)
+    z_go(2)
     for product in both:
         product.masks.relay()
-    z_go(2)
-    z_collect(0)
-    z_go(3)
-    z_collect(1)
+    collect(0)
+    z_go(4)
     for product in both:
         product.weights.relay()
+    collect(2, -2, 1, -1)
     for product in both:
         product.masks.far()
     flag_copies = [
@@ -397,13 +398,16 @@
     ]
     for cp in flag_copies:
         cp.start()
-    for k in range(4, RING // 2 + 1):
-        z_go(k)
-        z_collect(k - 2)
+    z_go(6)
+    collect(4, -4, 3, -3)
+    z_wait(8)
+    dispatch(8)
+    for d in (7, -7):
+        z_wait(d)
+    dispatch(7, -7)
     for product in both:
         product.weights.far()
-    z_collect(RING // 2 - 1)
-    z_collect(RING // 2)
+    collect(6, -6, 5, -5, 8, 7, -7)
     for cp in flag_copies:
         cp.wait()
 
@@ -428,144 +432,98 @@
         cp.wait_send()
 
 
-PARTS = 1
-CHAINS = 4
-LAG = 2
-EARLY = 0
-
-
-def tail_phase(
-    hid, d_own, d_far, o_ref, ha, hb, p, up_in, up_out, down_in, down_out, up_in16, up_out16, down_in16, down_out16,
-    gs, gr, ps, pr, us, ur, ds, dr, ls,
+CHAINS = 2
+
+
+def tail_phase(hid, d_own, d_far, o_ref, ha, hb, p, up_out, up_far, up_near, down_out, down_far, down_near,
+    as_, ar, bs, br, ps, pr, ufs, ufr, uns, unr, dfs, dfr, dns, dnr, ls,
 ):
     x, y, z, c = place()
-    up, down = device(x, y, wrap(z + 1, RING), c), device(x, y, wrap(z - 1, RING), c)
     other = device(x, y, z, 1 - c)
     me = y * SIDE + x
-    piece = ha.shape[2]
-    bit = piece // CHAINS
-    own = [
-        pltpu.make_async_copy(hid.at[c, pl.ds(q * piece, piece)], ha.at[q, me], ls.at[q]) for q in range(PARTS)
-    ]
-    for cp in own:
+    rows = ha.shape[1]
+    bit = rows // CHAINS
+    own = pltpu.make_async_copy(hid.at[c], ha.at[me], ls.at[0])
+    own.start()
+    swap = remote(hid.at[1 - c], hb.at[me], ps.at[0], pr.at[0], other)
+    swap.start()
+    own.wait()
+    a = Gather(ha, rows, True, as_, ar)
+    b = Gather(hb, rows, False, bs, br)
+    a.first()
+    a.second(0)
+    swap.wait_recv()
+    b.first()
+    b.second(0)
+    for s in (a, b):
+        s.relay()
+        s.second(1)
+        s.second(2)
+    for s in (a, b):
+        s.relay2(0)
+    for s in (a, b):
+        s.far()
+        s.second(3)
+    for i in (1, 2, 3):
+        for s in (a, b):
+            s.relay2(i)
+    for i in range(4):
+        for s in (a, b):
+            s.far2(i)
+    blocks, _, width = ha.shape
+    sums = jnp.dot(ha[...].reshape(blocks * rows, width), d_own[...], preferred_element_type=F32) + jnp.dot(
+        hb[...].reshape(blocks * rows, width), d_far[...], preferred_element_type=F32
+    )
+    p[...] = sums.reshape(p.shape)
+
+    ways = (
+        (1, RING // 2, up_out, up_far, up_near, ufs, ufr, uns, unr),
+        (-1, RING // 2 - 1, down_out, down_far, down_near, dfs, dfr, dns, dnr),
+    )
+    sends = []
+
+    def mine(sign, k, r):
+        return p[wrap(z + sign * k, RING), r * bit : (r + 1) * bit]
+
+    def hop(way, k, r):
+        sign, _, out, far, near, fs, fr, ns, nr = way
+        stop, step = (k - 2) // 2 if k % 2 == 0 else (k - 1) // 2, 2 - k % 2
+        dst, ss, rs = (near, ns, nr) if k % 2 else (far, fs, fr)
+        to = device(x, y, wrap(z + sign * step, RING), c)
+        return remote(out.at[k, r], dst.at[stop, r], ss.at[stop, r], rs.at[stop, r], to)
+
+    def push(way, k, r, value):
+        way[2][k, r] = value.astype(BF16)
+        cp = hop(way, k, r)
         cp.start()
-    swaps = [
-        remote(hid.at[1 - c, pl.ds(q * piece, piece)], hb.at[q, me], ps.at[q], pr.at[q], other) for q in range(PARTS)
-    ]
-    for cp in swaps:
-        cp.start()
-    for cp in own:
-        cp.wait()
-    a = [Gather(ha.at[q], piece, True, gs.at[q], gr.at[q]) for q in range(PARTS)]
-    b = [Gather(hb.at[q], piece, False, gs.at[PARTS + q], gr.at[PARTS + q]) for q in range(PARTS)]
-    sends = []
-    far_up, far_down = RING // 2, RING // 2 - 1
-
-    def begin(q):
-        a[q].first()
-        a[q].second(0)
-        swaps[q].wait_recv()
-        b[q].first()
-        b[q].second(0)
-
-    def near(q):
-        for s in (a[q], b[q]):
-            s.relay()
-            s.second(1)
-            s.second(2)
-
-    def middle(q):
-        for s in (a[q], b[q]):
-            s.relay2(0)
-        for s in (a[q], b[q]):
-            s.far()
-            s.second(3)
-
-    def late(q):
-        for i in (1, 2, 3):
-            for s in (a[q], b[q]):
-                s.relay2(i)
-
-    def ways(q, r):
-        n = q * CHAINS + r
-        return (
-            (up_in, up_out, up_in16, up_out16, up, us.at[n], ur.at[n], far_up, 1),
-            (down_in, down_out, down_in16, down_out16, down, ds.at[n], dr.at[n], far_down, -1),
-        )
-
-    def hop(k, n, way):
-        wide_in, wide_out, thin_in, thin_out, dev, ss, rs, _, _ = way
-        if k < EARLY:
-            return thin_out.at[k, n], remote(thin_out.at[k, n], thin_in.at[k, n], ss.at[k], rs.at[k], dev)
-        return wide_out.at[k - EARLY, n], remote(wide_out.at[k - EARLY, n], wide_in.at[k - EARLY, n], ss.at[k], rs.at[k], dev)
-
-    def arrived(k, n, way):
-        hop(k, n, way)[1].wait_recv()
-        return way[2][k, n].astype(F32) if k < EARLY else way[0][k - EARLY, n]
-
-    def mine(q, r, block):
-        return p[q, block, r * bit : (r + 1) * bit]
-
-    def end(q):
-        for i in range(4):
-            for s in (a[q], b[q]):
-                s.far2(i)
-
-    def multiply(q):
-        blocks, _, width = ha.shape[1:]
-        left = ha[q].reshape(blocks * piece, width)
-        right = hb[q].reshape(blocks * piece, width)
-        sums = jnp.dot(left, d_own[...], preferred_element_type=F32) + jnp.dot(
-            right, d_far[...], preferred_element_type=F32
-        )
-        p[q] = sums.reshape(p.shape[1:])
+        sends.append(cp)
+
+    def take(way, k, r, value):
+        far, near = way[3], way[4]
+        hop(way, k + 1, r).wait_recv()
+        value = value + near[k // 2, r].astype(F32)
+        if k + 2 <= way[1]:
+            hop(way, k + 2, r).wait_recv()
+            value = value + far[k // 2, r].astype(F32)
+        return value
+
+    for k in (8, 7, 5, 3, 1):
         for r in range(CHAINS):
-            n = q * CHAINS + r
-            for way in ways(q, r):
-                ref, cp = hop(0, n, way)
-                ref[...] = mine(q, r, wrap(z + way[-1] * way[-2], RING)).astype(ref.dtype)
-                cp.start()
-                sends.append(cp)
-
-    def step(k, q):
+            for way in ways:
+                if k <= way[1]:
+                    push(way, k, r, mine(way[0], k, r))
+    for k in (6, 4, 2):
         for r in range(CHAINS):
-            n = q * CHAINS + r
-            for way in ways(q, r):
-                far, sign = way[-2], way[-1]
-                if k < far:
-                    total = arrived(k - 1, n, way) + mine(q, r, wrap(z + sign * (far - k), RING))
-                    ref, cp = hop(k, n, way)
-                    ref[...] = total.astype(ref.dtype)
-                    cp.start()
-                    sends.append(cp)
-            if k == far_up:
-                total = mine(q, r, z)
-                for way in ways(q, r):
-                    total = total + arrived(way[-2] - 1, n, way)
-                row = q * piece + r * bit
-                o_ref[row : row + bit, :] = total.astype(BF16)
-
-    stages = (begin, near, middle, late, end, multiply)
-    at = [0] * PARTS
-    for tick in range(LAG * (PARTS - 1) + len(stages)):
-        for q in range(PARTS):
-            if at[q] and at[q] <= far_up:
-                step(at[q], q)
-                at[q] += 1
-        for q in range(PARTS):
-            n = tick - LAG * q
-            if 0 <= n < len(stages):
-                stages[n](q)
-                at[q] = int(n == len(stages) - 1)
-    while min(at) <= far_up:
-        for q in range(PARTS):
-            if at[q] <= far_up:
-                step(at[q], q)
-                at[q] += 1
-    for cp in swaps:
-        cp.wait_send()
-    for s in a + b:
-        s.drain()
+            for way in ways:
+                push(way, k, r, take(way, k, r, mine(way[0], k, r)))
+    for r in range(CHAINS):
+        total = mine(1, 0, r)
+        for way in ways:
+            total = take(way, 0, r, total)
+        o_ref[r * bit : (r + 1) * bit, :] = total.astype(BF16)
+    swap.wait_send()
+    a.drain()
+    b.drain()
     for cp in sends:
         cp.wait_send()
 
@@ -585,11 +543,9 @@
     rows, width = t.shape
     cols = d.shape[1]
     chips = SIDE * SIDE
-    n_up, n_down = RING // 2, RING // 2 - 1
     half = rows // 2
-    piece = half // PARTS
-    chains = PARTS * CHAINS
-    bit = piece // CHAINS
+    bit = half // CHAINS
+    stops = RING // 4
     product = [
         pltpu.VMEM((SIDE, PACK, BLK), BF16),
         pltpu.VMEM((SIDE, 2, SIDE, rows, width), BF16),
@@ -617,24 +573,22 @@
             pltpu.VMEM((SHARD, SHARD), BF16),
         ]
         + product * 2
-        + [dma((RING - 1, PIECES))] * 2
+        + [dma((RING - 1,))] * 2
         + [dma((1,))] * 2
         + [dma((6,))]
     )
     assert len(first) == N_FIRST
     last = (
         [
-            pltpu.VMEM((PARTS, chips, piece, SHARD), BF16),
-            pltpu.VMEM((PARTS, chips, piece, SHARD), BF16),
-            pltpu.VMEM((PARTS, chips, piece, cols), F32),
+            pltpu.VMEM((chips, half, SHARD), BF16),
+            pltpu.VMEM((chips, half, SHARD), BF16),
+            pltpu.VMEM((chips, half, cols), F32),
         ]
-        + [pltpu.VMEM((max(n - EARLY, 1), chains, bit, cols), F32) for n in (n_up, n_up, n_down, n_down)]
-        + [pltpu.VMEM((max(EARLY, 1), chains, bit, cols), BF16) for _ in range(4)]
-        + [dma((2 * PARTS, 20))] * 2
-        + [dma((PARTS,))] * 2
-        + [dma((chains, n_up))] * 2
-        + [dma((chains, n_down))] * 2
-        + [dma((PARTS,))]
+        + [pltpu.VMEM((n, CHAINS, bit, cols), BF16) for n in (RING // 2 + 1, stops, stops)] * 2
+        + [dma((20,))] * 4
+        + [dma((1,))] * 2
+        + [dma((stops, CHAINS))] * 8
+        + [dma((1,))]
     )
     out, _, _ = pl.pallas_call(
         layer_kernel,
@@ -650,7 +604,7 @@
             pl.BlockSpec(memory_space=HBM),
         ],
         scratch_shapes=kept + first + last,
-        compiler_params=pltpu.CompilerParams(collective_id=0, has_side_effects=True, vmem_limit_bytes=48 << 20),
+        compiler_params=pltpu.CompilerParams(collective_id=0, has_side_effects=True),
         name="layer",
     )(m, g, u, t, d)
     return out

time: 125 us -> 108 us (0.86)
  Pallas kernels: 121 us -> 105 us
  local copies, waits for them, and re-layouts: 4.22 us -> 1.47 us
    pallas_call x1, Pallas kernels: 117 us -> 102 us  [layer(): pl.pallas_call(layer_kernel, out_shape=[jax.ShapeDtypeStruct((half, cols)...]
    unnamed x11 -> x1, local copies, waits for them, and re-layouts: 4.22 us -> 1.47 us
where the time goes in v5:
time: 108 us; the launch traced here: 107 us
  Pallas kernels  105 us (97%)
  local copies, waits for them, and re-layouts  1.47 us (1%)
    pallas_call x1, Pallas kernels, layer(): pl.pallas_call(layer_kernel, out_shape=[jax.ShapeDtypeStruct((half, cols)...  102 us
    pallas_call x1, Pallas kernels, pack(): pl.pallas_call(pack_kernel, in_specs=[pl.BlockSpec(memory_space=pltpu.Mem...  3.22 us

profile of v5, /device:TPU:6, one launch (start us, length us, event | category | flops | bytes accessed | tf_op | source)
XLA Modules:
  0.0 106.7 jit_solution(4634661740661617226)
XLA Ops:
  0.0 3.2 %pack.1 = (s32[1,128]{1,0:T(1,128)}, bf16[1024,128]{1,0:T(8,128)(2,1)}, bf16[1024,128]{1,0:T(8,128)(2,1)}, bf16[512,512]{1,0:T(8,128)(2,1)}) custom-call(s32[4,4]{1,0:T(4,128)} %gk_ref.1, s32[4,4]{1,0:T(4,128)} %uk_ref.1, s32[4,4]{1,0:T(4,128)} %dk_ref.1, bf16[512,512]{1,0:T(8,128)(2,1)} %gw_in.1, bf16[512,512]{1,0:T(8,128)(2,1)} %uw_in.1, ...), custom_call_target="tpu_custom_call" | custom-call | tf_op jit(solution)/shard_map/pack/pallas_call | solution.py:172
  3.2 101.9 %layer.1 = (bf16[64,512]{1,0:T(8,128)(2,1)}, s32[4,1,128]{2,1,0:T(1,128)}, s32[4,1,128]{2,1,0:T(1,128)}) custom-call(s32[1,128]{1,0:T(1,128)} %get-tuple-element.10.refs_0_, bf16[1024,128]{1,0:T(8,128)(2,1)} %get-tuple-element.11.refs_1_, bf16[1024,128]{1,0:T(8,128)(2,1)} %get-tuple-element.12.refs_2_, bf16[128,256]{1,0:T(8,128)(2,1)} %refs_3_.1, ...), custom_call_target="tpu_custom_call" | custom-call | tf_op jit(solution)/shard_map/layer/pallas_call | solution.py:593
  105.2 1.5 %copy.9 = bf16[64,512]{1,0:T(8,128)(2,1)} copy(bf16[64,512]{1,0:T(8,128)(2,1)} %get-tuple-element.14) | data formatting | bytes 131072

commit v6 on v5

--- a/solution.py
+++ b/solution.py
@@ -45,10 +45,11 @@
 
 
 class Gather:
+    relayed = False
+
     def __init__(self, buf, rows, x_first, send, recv):
         x, y, z, c = place()
         self.buf, self.send, self.recv = buf, send, recv
-        self.split = rows > 1
         self.pieces = (pl.ds(0, rows // 2), pl.ds(rows // 2, rows // 2))
         self.a, self.b = (x, y) if x_first else (y, x)
         self.slot = lambda a, b: (b * SIDE + a) if x_first else (a * SIDE + b)
@@ -90,21 +91,26 @@
         s = self.slot(self.a, self.b)
         self.copy("r", 0, s, None, self.dev(wrap(self.a + 1, SIDE), self.b))
         self.copy("l", 1, s, None, self.dev(wrap(self.a - 1, SIDE), self.b))
+        if not self.relayed:
+            self.copy("f", 2, s, None, self.dev(wrap(self.a + 2, SIDE), self.b))
 
     def relay(self):
         left = self.slot(wrap(self.a - 1, SIDE), self.b)
         right = self.slot(wrap(self.a + 1, SIDE), self.b)
         self.got(0, left, None)
-        self.copy("fr", 2, left, 0 if self.split else None, self.dev(wrap(self.a + 1, SIDE), self.b))
+        if self.relayed:
+            self.copy("fr", 2, left, 0, self.dev(wrap(self.a + 1, SIDE), self.b))
         self.got(1, right, None)
-        if self.split:
+        if self.relayed:
             self.copy("fl", 3, right, 1, self.dev(wrap(self.a - 1, SIDE), self.b))
 
     def far(self):
         opposite = self.slot(wrap(self.a + 2, SIDE), self.b)
-        self.got(2, opposite, 0 if self.split else None)
-        if self.split:
+        if self.relayed:
+            self.got(2, opposite, 0)
             self.got(3, opposite, 1)
+        else:
+            self.got(2, opposite, None)
 
     OFF = (0, -1, 1, 2)
 
@@ -119,17 +125,15 @@
         below = self.slot(a, wrap(self.b - 1, SIDE))
         above = self.slot(a, wrap(self.b + 1, SIDE))
         self.got(4 + 4 * i, below, None)
-        self.copy(("fu", i), 6 + 4 * i, below, 0 if self.split else None, self.dev(self.a, wrap(self.b + 1, SIDE)))
+        self.copy(("fu", i), 6 + 4 * i, below, 0, self.dev(self.a, wrap(self.b + 1, SIDE)))
         self.got(5 + 4 * i, above, None)
-        if self.split:
-            self.copy(("fd", i), 7 + 4 * i, above, 1, self.dev(self.a, wrap(self.b - 1, SIDE)))
+        self.copy(("fd", i), 7 + 4 * i, above, 1, self.dev(self.a, wrap(self.b - 1, SIDE)))
 
     def far2(self, i):
         a = wrap(self.a + self.OFF[i], SIDE)
         s = self.slot(a, wrap(self.b + 2, SIDE))
-        self.got(6 + 4 * i, s, 0 if self.split else None)
-        if self.split:
-            self.got(7 + 4 * i, s, 1)
+        self.got(6 + 4 * i, s, 0)
+        self.got(7 + 4 * i, s, 1)
 
     def drain(self):
         for cp in self.copies.values():
@@ -194,6 +198,7 @@
     def __init__(self, buf, rows, along_x, send, recv):
         super().__init__(buf, rows, along_x, send, recv)
         self.slot = lambda a, b: a
+        self.relayed = rows > 1
 
 
 class Product:
@@ -237,23 +242,26 @@
             half = self.t.at[j, place()[3]]
             remote(half, half, self.hs.at[j], self.hr.at[j], other).start()
 
-    def multiply(self, j, other, stage, dense):
-        half = self.t.at[j, 1 - place()[3]]
-        remote(half, half, self.hs.at[j], self.hr.at[j], other).wait_recv()
+    def multiply(self, j, p, stage, dense):
         stage[...] = self.w[j].reshape(stage.shape)
+        half = NB // 2
         rank = jnp.int32(0)
-        for n in range(NB * NB):
+        for n in range(half * NB):
+            rank = rank + self.flags[j, 0, self.lane + n]
+        rank = rank * p
+        for n in range(half * NB):
             r, q = n // NB, n % NB
-            keep = self.flags[j, 0, self.lane + n]
+            keep = self.flags[j, 0, self.lane + p * half * NB + n]
             tile = stage[jnp.minimum(rank, CAP - 1)]
             dense[r * BLK : (r + 1) * BLK, q * BLK : (q + 1) * BLK] = tile * keep.astype(F32).astype(BF16)
             rank = rank + keep
         _, _, lines, rows, width = self.t.shape
-        left, right = self.t[j, 0].reshape(lines * rows, width), self.t[j, 1].reshape(lines * rows, width)
-        self.acc[...] += (
-            jnp.dot(left, dense[:width], preferred_element_type=F32)
-            + jnp.dot(right, dense[width:], preferred_element_type=F32)
-        ).reshape(self.acc.shape)
+        features = self.t[j, p].reshape(lines * rows, width)
+        self.acc[...] += jnp.dot(features, dense[...], preferred_element_type=F32).reshape(self.acc.shape)
+
+    def shared(self, j, other):
+        half = self.t.at[j, 1 - place()[3]]
+        remote(half, half, self.hs.at[j], self.hr.at[j], other).wait_recv()
 
     def sum_copy(self, n):
         a, rows = self.a, self.acc.shape[1] // 2
@@ -415,8 +423,15 @@
 
         @pl.loop(0, SIDE)
         def _(n, product=product):
+            product.multiply(wrap(lax.div(z, SIDE) + n, SIDE), c, stage, dense)
+
+    for product in both:
+
+        @pl.loop(0, SIDE)
+        def _(n, product=product):
             j = wrap(lax.div(z, SIDE) + n, SIDE)
-            product.multiply(j, other, stage, dense)
+            product.shared(j, other)
+            product.multiply(j, 1 - c, stage, dense)
 
         if product is up_:
             gate.sum_relay()
@@ -460,11 +475,9 @@
         s.second(1)
         s.second(2)
     for s in (a, b):
-        s.relay2(0)
-    for s in (a, b):
         s.far()
         s.second(3)
-    for i in (1, 2, 3):
+    for i in range(4):
         for s in (a, b):
             s.relay2(i)
     for i in range(4):
@@ -570,7 +583,7 @@
         [
             pltpu.VMEM((RING, rows, width), BF16),
             pltpu.VMEM((CAP, BLK, BLK), BF16),
-            pltpu.VMEM((SHARD, SHARD), BF16),
+            pltpu.VMEM((SHARD // 2, SHARD), BF16),
         ]
         + product * 2
         + [dma((RING - 1,))] * 2

time: 108 us -> 110 us (1.019)
  Pallas kernels: 105 us -> 107 us
    pallas_call x1, Pallas kernels: 102 us -> 104 us  [layer(): pl.pallas_call(layer_kernel, out_shape=[jax.ShapeDtypeStruct((half, cols)...]
where the time goes in v6:
time: 110 us; the launch traced here: 109 us
  Pallas kernels  107 us (97%)
  local copies, waits for them, and re-layouts  1.47 us (1%)
    pallas_call x1, Pallas kernels, layer(): pl.pallas_call(layer_kernel, out_shape=[jax.ShapeDtypeStruct((half, cols)...  104 us
    pallas_call x1, Pallas kernels, pack(): pl.pallas_call(pack_kernel, in_specs=[pl.BlockSpec(memory_space=pltpu.Mem...  3.21 us

profile of v6, /device:TPU:6, one launch (start us, length us, event | category | flops | bytes accessed | tf_op | source)
XLA Modules:
  0.0 108.8 jit_solution(671603012489071754)
XLA Ops:
  0.0 3.2 %pack.1 = (s32[1,128]{1,0:T(1,128)}, bf16[1024,128]{1,0:T(8,128)(2,1)}, bf16[1024,128]{1,0:T(8,128)(2,1)}, bf16[512,512]{1,0:T(8,128)(2,1)}) custom-call(s32[4,4]{1,0:T(4,128)} %gk_ref.1, s32[4,4]{1,0:T(4,128)} %uk_ref.1, s32[4,4]{1,0:T(4,128)} %dk_ref.1, bf16[512,512]{1,0:T(8,128)(2,1)} %gw_in.1, bf16[512,512]{1,0:T(8,128)(2,1)} %uw_in.1, ...), custom_call_target="tpu_custom_call" | custom-call | tf_op jit(solution)/shard_map/pack/pallas_call | solution.py:176
  3.2 104.1 %layer.1 = (bf16[64,512]{1,0:T(8,128)(2,1)}, s32[4,1,128]{2,1,0:T(1,128)}, s32[4,1,128]{2,1,0:T(1,128)}) custom-call(s32[1,128]{1,0:T(1,128)} %get-tuple-element.10.refs_0_, bf16[1024,128]{1,0:T(8,128)(2,1)} %get-tuple-element.11.refs_1_, bf16[1024,128]{1,0:T(8,128)(2,1)} %get-tuple-element.12.refs_2_, bf16[128,256]{1,0:T(8,128)(2,1)} %refs_3_.1, ...), custom_call_target="tpu_custom_call" | custom-call | tf_op jit(solution)/shard_map/layer/pallas_call | solution.py:606
  107.3 1.5 %copy.9 = bf16[64,512]{1,0:T(8,128)(2,1)} copy(bf16[64,512]{1,0:T(8,128)(2,1)} %get-tuple-element.14) | data formatting | bytes 131072
